TPU v7x, 32 devices: a whole 2x2x4 slice. The times are simulated.
32 devices in a mesh: gx: 4 (over y, core), gy: 4 (over z), gz: 2 (over x).
Axes of the slice: x: 2, y: 2, z: 4, core: 2. Of those that a mesh axis runs over, the one named last changes fastest.
Arguments:
- gas_state: float32 [5, 32, 64, 256], P(None, 'gx', 'gy', 'gz'), may hold values from -6 to 6, as said below
- section_start: float32 [5, 32, 64, 256], P(None, 'gx', 'gy', 'gz'), may hold values from -6 to 6
- drop_cell: int32 [4, 4, 2, 16, 128], P('gx', 'gy', 'gz'), may hold values from 0 to 8191
- block_tile: int32 [4, 4, 2, 16], P('gx', 'gy', 'gz'), may hold values from 0 to 1, as said below
- droplets_per_block: int32 [4, 4, 2, 16], P('gx', 'gy', 'gz'), may hold values from 0 to 128, as said below
- drop_frac: float32 [4, 4, 2, 3, 16, 128], P('gx', 'gy', 'gz'), may hold values from -0.5 to 0.5
- drop_vel: float32 [4, 4, 2, 3, 16, 128], P('gx', 'gy', 'gz'), may hold values from -6 to 6
- drop_mass: float32 [4, 4, 2, 16, 128], P('gx', 'gy', 'gz'), may hold values from 0.1 to 4
- drop_temp: float32 [4, 4, 2, 16, 128], P('gx', 'gy', 'gz'), may hold values from -6 to 6
Outputs:
- new_state: float32 [5, 32, 64, 256], P(None, 'gx', 'gy', 'gz')
Inputs may be any that keep to these rules, and one draw needn't show every extreme that they name: `gas_state`: component 0 (density) lies between 0.3 and 3.4. `drop_cell`: encodes the cell (x, y, z) within the block's tile as (x * 8 + y) * 128 + z. `block_tile`: nondecreasing along a device's blocks; blocks with count 0 carry tile 1 (the last tile). `droplets_per_block`: on each device the blocks with a positive count come first and every later block has count 0; each device has at least 4 live blocks, one of them with 128 droplets; some device has all 16 blocks live. Slot d of a block is live when d is below its count.
All inputs are finite; a program needn't handle non-finite values.
Results may differ from a plain program's by a relative error of at most 0.00057.
Values sent between devices are 32-bit elements; how exact they have to be, the bound alone decides.
A program may use at most 64 MiB of HBM per device.

v0:
```python
import math

import jax
import jax.numpy as jnp
from jax import lax
from jax.sharding import PartitionSpec as P

TS = 8


PARCEL = 8.0
LATENT = 0.5
TIME_INCREMENT = 0.2
VISCOSITY = 0.5


def with_halo(cells, sides, width):
    for axis, dim in sides:
        count = lax.axis_size(axis)
        head = lax.slice_in_dim(cells, 0, width, axis=dim)
        tail = lax.slice_in_dim(cells, cells.shape[dim] - width, cells.shape[dim], axis=dim)
        cells = jnp.concatenate(
            [
                lax.ppermute(tail, axis, [(i, (i + 1) % count) for i in range(count)]),
                cells,
                lax.ppermute(head, axis, [((i + 1) % count, i) for i in range(count)]),
            ],
            axis=dim,
        )
    return cells


def cut_windows(values, tile_size):
    number = (values.shape[0] - 2) // tile_size
    trailing = values.shape[1:]
    rest_pad = [(0, 0)] * len(trailing)
    leading = values[: number * tile_size].reshape((number, tile_size) + trailing)
    upper_rows = jnp.pad(values[tile_size:], [(0, tile_size - 2)] + rest_pad)
    upper_rows = upper_rows.reshape((number, tile_size) + trailing)[:, :2]
    return jnp.concatenate([leading, upper_rows], axis=1)


def join_windows(values, tile_size):
    number = values.shape[0]
    trailing = values.shape[2:]
    rest_pad = [(0, 0)] * len(trailing)
    leading = values[:, :tile_size].reshape((number * tile_size,) + trailing)
    leading = jnp.pad(leading, [(0, 2)] + rest_pad)
    upper_rows = jnp.pad(values[:, tile_size:], [(0, 0), (0, tile_size - 2)] + rest_pad)
    upper_rows = upper_rows.reshape((number * tile_size,) + trailing)
    upper_rows = jnp.pad(upper_rows, [(tile_size, 0)] + rest_pad)[: number * tile_size + 2]
    return leading + upper_rows


def tile_footprints(padded, tile_size):
    arranged = cut_windows(jnp.moveaxis(padded, 1, 0), tile_size)
    arranged = cut_windows(jnp.moveaxis(arranged, 3, 0), tile_size)
    arranged = jnp.transpose(arranged, (2, 0, 4, 3, 1, 5))
    return arranged.reshape(arranged.shape[0] * arranged.shape[1], -1, arranged.shape[5])


def tiles_to_padded(tile_sums, tiles_x, tile_rows_along_y, components, tile_size):
    foot_width = tile_size + 2
    arranged = tile_sums.reshape(
        tiles_x, tile_rows_along_y, components, foot_width, foot_width, tile_sums.shape[2]
    )
    arranged = jnp.transpose(arranged, (0, 3, 1, 4, 2, 5))
    arranged = join_windows(arranged, tile_size)
    arranged = join_windows(jnp.moveaxis(arranged, 0, 2), tile_size)
    return jnp.transpose(arranged, (2, 1, 0, 3))


def spread(position, offset, length):
    places = jnp.arange(length, dtype=jnp.int32)[None, :, None]
    anchor = position[:, None, :]
    low_weight = (0.5 * (0.5 - offset) * (0.5 - offset))[:, None, :]
    middle = (0.75 - offset * offset)[:, None, :]
    higher = (0.5 * (0.5 + offset) * (0.5 + offset))[:, None, :]
    return (
        jnp.where(places == anchor, low_weight, 0.0)
        + jnp.where(places == anchor + 1, middle, 0.0)
        + jnp.where(places == anchor + 2, higher, 0.0)
    )


def block_weights(drop_cells, offsets, tile_size, cells_z):
    plane_size = tile_size * cells_z
    pos_x = drop_cells // plane_size
    pos_y = drop_cells // cells_z % tile_size
    pos_z = drop_cells % cells_z
    foot_width = tile_size + 2
    weight_x = spread(pos_x, offsets[0], foot_width)
    weight_y = spread(pos_y, offsets[1], foot_width)
    planar = (weight_x[:, :, None, :] * weight_y[:, None, :, :]).reshape(
        drop_cells.shape[0], foot_width * foot_width, drop_cells.shape[1]
    )
    upward_direction = spread(pos_z, offsets[2], cells_z + 2)
    return (planar, upward_direction)


def droplet_terms(gas_at, velocity, masses, temper, counts):
    slots = jnp.arange(masses.shape[1], dtype=jnp.int32)[None, :]
    alive_weight = jnp.where(slots < counts[:, None], PARCEL, 0.0)
    diameter = jnp.cbrt(masses)
    spalding = jax.nn.softplus(gas_at[:, 4] - temper)
    evaporation = diameter * jnp.log1p(spalding)
    drag_force = (diameter * gas_at[:, 0])[:, None, :] * (gas_at[:, 1:4] - velocity)
    heat_flux = diameter * (gas_at[:, 4] - temper)
    momentum = evaporation[:, None, :] * velocity - drag_force
    energy = -heat_flux - LATENT * evaporation
    stacked = jnp.concatenate([evaporation[:, None, :], momentum, energy[:, None, :]], axis=1)
    return stacked * alive_weight[:, None, :]


def neighbour(padded, dim_index, offset):
    slicer = [slice(None), slice(1, -1), slice(1, -1), slice(1, -1)]
    length = padded.shape[dim_index] - 2
    slicer[dim_index] = slice(1 + offset, 1 + offset + length)
    return padded[tuple(slicer)]


def advance(padded, gas_state, section_start, sources):
    laplace = -6.0 * gas_state
    advect = jnp.zeros_like(gas_state)
    for dim_index in (1, 2, 3):
        higher = neighbour(padded, dim_index, 1)
        lower_cells = neighbour(padded, dim_index, -1)
        laplace = laplace + higher + lower_cells
        advect = advect + gas_state[dim_index][None] * (higher - lower_cells) * 0.5
    return 0.75 * section_start + 0.25 * (
        gas_state + TIME_INCREMENT * (VISCOSITY * laplace - advect + sources)
    )


def fold_rim(values, dim_index):
    moved_axis = jnp.moveaxis(values, dim_index, 0)
    core_cells = moved_axis[2:-2].at[0].add(moved_axis[0]).at[-1].add(moved_axis[-1])
    return jnp.moveaxis(core_cells, 0, dim_index)


def local(
    gas_state,
    section_start,
    drop_cell,
    block_tile,
    droplets_per_block,
    drop_frac,
    drop_vel,
    drop_mass,
    drop_temp,
):
    components, cells_x, cells_y, cells_z = gas_state.shape
    padded = with_halo(gas_state, (("gx", 1), ("gy", 2), ("gz", 3)), 1)
    footprints = tile_footprints(padded.astype(jnp.bfloat16), TS)
    drop_cells = drop_cell.reshape(drop_cell.shape[3:])
    tile_ids = block_tile.reshape(block_tile.shape[3:])
    counts = droplets_per_block.reshape(droplets_per_block.shape[3:])
    offsets = drop_frac.reshape(drop_frac.shape[3:])
    velocity = drop_vel.reshape(drop_vel.shape[3:])
    masses = drop_mass.reshape(drop_mass.shape[3:])
    temper = drop_temp.reshape(drop_temp.shape[3:])
    blocks, block_size = drop_cells.shape
    group_size = math.gcd(blocks, 8)
    tile_count = footprints.shape[0]
    owners_table = jnp.arange(tile_count, dtype=jnp.int32)[None, :]

    def deposit_group(turn_index, running):
        first_block = turn_index * group_size

        def window(values, dim_index):
            return lax.dynamic_slice_in_dim(values, first_block, group_size, dim_index)

        group_ids = window(tile_ids, 0)
        planar, upward_direction = block_weights(
            window(drop_cells, 0), window(offsets, 1), TS, cells_z
        )
        planar = planar.astype(jnp.bfloat16)
        upward_direction = upward_direction.astype(jnp.bfloat16)
        source_portions = jnp.take(footprints, group_ids, axis=0)
        nearby_gas_values = jnp.einsum(
            "gsy,gyn->gsn", source_portions, upward_direction, preferred_element_type=jnp.float32
        )
        gas_at = jnp.sum(
            nearby_gas_values.reshape(group_size, components, -1, block_size) * planar[:, None],
            axis=2,
        )
        sources = droplet_terms(
            gas_at,
            jnp.transpose(window(velocity, 1), (1, 0, 2)),
            window(masses, 0),
            window(temper, 0),
            window(counts, 0),
        )
        weight_scaled_terms = (
            (planar[:, None] * sources[:, :, None, :])
            .astype(jnp.bfloat16)
            .reshape(group_size, -1, block_size)
        )
        spread_sources = jnp.einsum(
            "peh,pch->pec",
            weight_scaled_terms,
            upward_direction,
            preferred_element_type=jnp.float32,
        )
        owners = (group_ids[:, None] == owners_table).astype(jnp.float32)
        return running + jnp.einsum(
            "bt,bkz->tkz", owners, spread_sources, precision=lax.Precision.HIGHEST
        )

    start_sums = jnp.zeros((tile_count,) + footprints.shape[1:], jnp.float32)
    turn_count = blocks // group_size
    tile_sums = lax.fori_loop(0, turn_count, deposit_group, start_sums)
    spread_sources = tiles_to_padded(tile_sums, cells_x // TS, cells_y // TS, components, TS)
    extended = with_halo(spread_sources, (("gx", 1), ("gy", 2), ("gz", 3)), 1)
    sources = fold_rim(fold_rim(fold_rim(extended, 1), 2), 3)
    return advance(padded, gas_state, section_start, sources)


def solution(mesh):
    in_specs = (
        P(None, "gx", "gy", "gz"),
        P(None, "gx", "gy", "gz"),
        P("gx", "gy", "gz", None, None),
        P("gx", "gy", "gz", None),
        P("gx", "gy", "gz", None),
        P("gx", "gy", "gz", None, None, None),
        P("gx", "gy", "gz", None, None, None),
        P("gx", "gy", "gz", None, None),
        P("gx", "gy", "gz", None, None),
    )
    out_specs = P(None, "gx", "gy", "gz")
    return jax.shard_map(local, mesh=mesh, in_specs=in_specs, out_specs=out_specs, check_vma=False)
```

profile of v0, /device:TPU:0, one launch (start us, length us, event | category | flops | bytes accessed | tf_op | source)
XLA Modules:
  0.0 80.7 jit_solution(8475079953495699244)
XLA Ops:
  0.0 0.8 fusion.45
  0.8 0.5 collective-permute-start.1
  1.3 2.0 %collective-permute-start = (f32[5,1,16,128]{3,2,0,1:T(8,128)S(1)}, f32[5,1,16,128]{3,2,0,1:T(8,128)S(1)}, u32[]{:S(2)}, u32[]{:S(2)}) collective-permute-start(f32[5,1,16,128]{3,2,0,1:T(8,128)S(1)} %get-tuple-element.521), channel_id=1, source_target_pairs={{8,0},{16,8},{24,16},{0,24},{9,1},{17,9},{25,17},{1,25},{10,2},{18... | collective-permute-start | bytes 122888 | tf_op jit(solution)/shard_map/ppermute | solution.py:26
  3.3 1.6 %collective-permute-done.1 = f32[5,1,16,128]{3,2,0,1:T(8,128)S(1)} collective-permute-done((f32[5,1,16,128]{3,2,0,1:T(8,128)S(1)}, f32[5,1,16,128]{3,2,0,1:T(8,128)S(1)}, u32[]{:S(2)}, u32[]{:S(2)}) %collective-permute-start.1) | collective-permute-done | bytes 40992 | tf_op jit(solution)/shard_map/ppermute | solution.py:24
  4.9 1.0 %constant_dynamic-update-slice_fusion.1 = f32[5,10,16,128]{3,2,0,1:T(8,128)S(1)} fusion(f32[5,10,16,128]{3,2,0,1:T(8,128)S(1)} %constant_dynamic-update-slice_fusion.2, f32[5,8,16,128]{3,2,1,0:T(8,128)} %param.23), kind=kLoop, calls=%fused_computation.135 | loop fusion | bytes 655360
  6.0 4.4 %collective-permute-start.2 = (f32[5,10,1,128]{3,2,0,1:T(1,128)S(1)}, f32[5,10,1,128]{3,2,0,1:T(1,128)S(1)}, u32[]{:S(2)}, u32[]{:S(2)}) collective-permute-start(f32[5,10,1,128]{3,2,0,1:T(1,128)S(1)} %get-tuple-element.517), channel_id=1, source_target_pairs={{2,0},{4,2},{6,4},{0,6},{3,1},{5,3},{7,5},{1,7},{10,8},{12,10},{14... | collective-permute-start | bytes 76808 | tf_op jit(solution)/shard_map/ppermute | solution.py:26
  10.5 1.5 %collective-permute-done.2 = f32[5,10,1,128]{3,2,0,1:T(1,128)S(1)} collective-permute-done((f32[5,10,1,128]{3,2,0,1:T(1,128)S(1)}, f32[5,10,1,128]{3,2,0,1:T(1,128)S(1)}, u32[]{:S(2)}, u32[]{:S(2)}) %collective-permute-start.2) | collective-permute-done | bytes 25632 | tf_op jit(solution)/shard_map/ppermute | solution.py:26
  12.0 4.1 %collective-permute-done.3 = f32[5,10,1,128]{3,2,0,1:T(1,128)S(1)} collective-permute-done((f32[5,10,1,128]{3,2,0,1:T(1,128)S(1)}, f32[5,10,1,128]{3,2,0,1:T(1,128)S(1)}, u32[]{:S(2)}, u32[]{:S(2)}) %collective-permute-start.3) | collective-permute-done | bytes 25632 | tf_op jit(solution)/shard_map/ppermute | solution.py:24
  16.8 1.5 %collective-permute-start.5 = (f32[5,10,18,1]{2,3,1,0:T(1,128)S(1)}, f32[5,10,18,1]{2,3,1,0:T(1,128)S(1)}, u32[]{:S(2)}, u32[]{:S(2)}) collective-permute-start(f32[5,10,18,1]{2,3,1,0:T(1,128)S(1)} %copy.81), channel_id=1, source_target_pairs={{0,1},{1,0},{2,3},{3,2},{4,5},{5,4},{6,7},{7,6},{8,9},{9,8},{10,11... | collective-permute-start | bytes 10808 | tf_op jit(solution)/shard_map/ppermute | solution.py:24
  18.8 0.6 collective-permute-start.4
  19.5 1.4 %collective-permute-done.5 = f32[5,10,18,1]{2,3,1,0:T(1,128)S(1)} collective-permute-done((f32[5,10,18,1]{2,3,1,0:T(1,128)S(1)}, f32[5,10,18,1]{2,3,1,0:T(1,128)S(1)}, u32[]{:S(2)}, u32[]{:S(2)}) %collective-permute-start.5) | collective-permute-done | bytes 3632 | tf_op jit(solution)/shard_map/ppermute | solution.py:24
  21.3 1.4 %collective-permute-done.4 = f32[5,10,18,1]{2,3,1,0:T(1,128)S(1)} collective-permute-done((f32[5,10,18,1]{2,3,1,0:T(1,128)S(1)}, f32[5,10,18,1]{2,3,1,0:T(1,128)S(1)}, u32[]{:S(2)}, u32[]{:S(2)}) %collective-permute-start.4) | collective-permute-done | bytes 3632 | tf_op jit(solution)/shard_map/ppermute | solution.py:26
  24.5 0.7 pad_maximum_fusion.2
  25.4 12.6 %while.23 = (s32[]{:T(128)}, f32[2,500,130]{1,0,2:T(2,128)S(1)}, s32[16]{0:T(128)S(1)}, s32[16,128]{1,0:T(8,128)S(1)}, f32[3,16,128]{2,1,0:T(8,128)S(1)}, /*inde...) while((s32[]{:T(128)}, f32[2,500,130]{1,0,2:T(2,128)S(1)}, ...), condition=%wide.region_2.3_spmd.clone, body=%wide.region_0.2_spmd.clone.sunk | while | flops 284528960 | bytes 20749924 | solution.py:212
  25.6 0.7 gather_fusion
  26.3 0.8 fusion.60
  28.2 0.8 %fusion.63 = f32[8,500,130]{1,2,0:T(8,128)S(1)} fusion(bf16[8,500,128]{2,0,1:T(8,128)(2,1)S(1)} %bitcast.126, f32[8,128]{1,0:T(8,128)S(1)} %get-tuple-element.611, s32[8,128]{1,0:T(8,128)S(1)} %broadcast_add_fusion.13, f32[8,128]{1,0:T(8,128)S(1)} %get-tuple-element.614, s32[8,128]{1,0:T(8,128)S(1)} %get-tuple-element.615, ...), kind=kOutput, calls=%fused_computation.10.clone.1 | convolution fusion | flops 134318080 | bytes 3128576 | tf_op jit(solution)/shard_map/while/body/eval_jaxpr/peh,pch->pec/dot_general | solution.py:199
  29.0 2.7 %fusion.64 = f32[2,500,130]{1,0,2:T(2,128)S(1)} fusion(f32[8,500,130]{1,2,0:T(8,128)S(1)} %fusion.63, f32[2,500,130]{1,0,2:T(2,128)S(1)} %get-tuple-element.649, pred[]{:T(512)S(6)} %compare.65, s32[8]{0:T(128)S(1)} %get-tuple-element.609), kind=kOutput, calls=%fused_computation.9.clone.1 | convolution fusion | flops 12740016 | bytes 3120033 | tf_op jit(solution)/shard_map/while/body/eval_jaxpr/bt,bkz->tkz/dot_general | solution.py:206
  31.9 0.7 gather_fusion
  32.6 0.8 fusion.60
  34.5 0.8 %fusion.63 = f32[8,500,130]{1,2,0:T(8,128)S(1)} fusion(bf16[8,500,128]{2,0,1:T(8,128)(2,1)S(1)} %bitcast.126, f32[8,128]{1,0:T(8,128)S(1)} %get-tuple-element.611, s32[8,128]{1,0:T(8,128)S(1)} %broadcast_add_fusion.13, f32[8,128]{1,0:T(8,128)S(1)} %get-tuple-element.614, s32[8,128]{1,0:T(8,128)S(1)} %get-tuple-element.615, ...), kind=kOutput, calls=%fused_computation.10.clone.1 | convolution fusion | flops 134318080 | bytes 3128576 | tf_op jit(solution)/shard_map/while/body/eval_jaxpr/peh,pch->pec/dot_general | solution.py:199
  35.3 2.7 %fusion.64 = f32[2,500,130]{1,0,2:T(2,128)S(1)} fusion(f32[8,500,130]{1,2,0:T(8,128)S(1)} %fusion.63, f32[2,500,130]{1,0,2:T(2,128)S(1)} %get-tuple-element.649, pred[]{:T(512)S(6)} %compare.65, s32[8]{0:T(128)S(1)} %get-tuple-element.609), kind=kOutput, calls=%fused_computation.9.clone.1 | convolution fusion | flops 12740016 | bytes 3120033 | tf_op jit(solution)/shard_map/while/body/eval_jaxpr/bt,bkz->tkz/dot_general | solution.py:206
  38.0 1.3 %copy.90 = f32[2,500,130]{2,0,1:T(2,128)S(1)} copy(f32[2,500,130]{1,0,2:T(2,128)S(1)} %get-tuple-element.387) | data formatting | bytes 1040000 | tf_op jit(solution)/shard_map/while | solution.py:212
  39.3 0.5 slice_bitcast_fusion.2
  40.3 0.5 slice.437
  41.3 1.7 %collective-permute-start.7 = (f32[5,1,18,130]{3,2,0,1:T(8,128)S(1)}, f32[5,1,18,130]{3,2,0,1:T(8,128)S(1)}, u32[]{:S(2)}, u32[]{:S(2)}) collective-permute-start(f32[5,1,18,130]{3,2,0,1:T(8,128)S(1)} %get-tuple-element.513), channel_id=1, source_target_pairs={{8,0},{16,8},{24,16},{0,24},{9,1},{17,9},{25,17},{1,25},{10,2},{18... | collective-permute-start | bytes 140408 | tf_op jit(solution)/shard_map/ppermute | solution.py:26
  43.1 2.6 %collective-permute-done.6 = f32[5,1,18,130]{3,2,0,1:T(8,128)S(1)} collective-permute-done((f32[5,1,18,130]{3,2,0,1:T(8,128)S(1)}, f32[5,1,18,130]{3,2,0,1:T(8,128)S(1)}, u32[]{:S(2)}, u32[]{:S(2)}) %collective-permute-start.6) | collective-permute-done | bytes 46832 | tf_op jit(solution)/shard_map/ppermute | solution.py:24
  46.2 3.8 %collective-permute-start.9 = (f32[5,12,1,130]{3,2,0,1:T(1,128)S(1)}, f32[5,12,1,130]{3,2,0,1:T(1,128)S(1)}, u32[]{:S(2)}, u32[]{:S(2)}) collective-permute-start(f32[5,12,1,130]{3,2,0,1:T(1,128)S(1)} %get-tuple-element.511), channel_id=1, source_target_pairs={{2,0},{4,2},{6,4},{0,6},{3,1},{5,3},{7,5},{1,7},{10,8},{12,10},{14... | collective-permute-start | bytes 93608 | tf_op jit(solution)/shard_map/ppermute | solution.py:26
  50.0 2.6 %collective-permute-done.8 = f32[5,12,1,130]{3,2,0,1:T(1,128)} collective-permute-done((f32[5,12,1,130]{3,2,0,1:T(1,128)S(1)}, f32[5,12,1,130]{3,2,0,1:T(1,128)}, u32[]{:S(2)}, u32[]{:S(2)}) %collective-permute-start.8) | collective-permute-done | bytes 31232 | tf_op jit(solution)/shard_map/ppermute | solution.py:24
  52.6 0.6 copy-done.8
  53.2 1.1 %pad_maximum_fusion = f32[5,12,20,130]{3,2,0,1:T(8,128)S(1)} fusion(f32[5,12,1,130]{3,2,0,1:T(1,128)S(1)} %collective-permute-done.9, f32[5,1,18,130]{3,2,0,1:T(8,128)S(1)} %collective-permute-done.7, f32[5,10,18,130]{3,2,0,1:T(8,128)S(1)} %add_bitcast_fusion, f32[5,1,18,130]{3,2,0,1:T(8,128)S(1)} %collective-permute-done.6, ...), kind=kLoop, calls=%fused_computation.85 | loop fusion | flops 624000 | bytes 1248000 | tf_op jit(solution)/shard_map/concatenate | solution.py:22
  54.6 1.0 %copy.93 = f32[5,12,20,1]{2,3,1,0:T(1,128)} copy(f32[5,12,20,1]{3,2,0,1:T(8,128)S(1)} %get-tuple-element.508) | data formatting | bytes 9600 | tf_op jit(solution)/shard_map/slice | solution.py:21
  55.7 0.6 collective-permute-start.10
  56.2 0.5 copy.94
  56.7 1.5 %collective-permute-start.11 = (f32[5,12,20,1]{2,3,1,0:T(1,128)S(1)}, f32[5,12,20,1]{2,3,1,0:T(1,128)}, u32[]{:S(2)}, u32[]{:S(2)}) collective-permute-start(f32[5,12,20,1]{2,3,1,0:T(1,128)S(1)} %copy.94), channel_id=1, source_target_pairs={{1,0},{0,1},{3,2},{2,3},{5,4},{4,5},{7,6},{6,7},{9,8},{8,9},{11,10... | collective-permute-start | bytes 14408 | tf_op jit(solution)/shard_map/ppermute | solution.py:26
  58.2 0.7 slice_bitcast_fusion.7
  58.9 0.7 copy.97
  59.6 1.2 %copy.80 = f32[5,10,18,1]{3,2,0,1:T(8,128)S(1)} copy(f32[5,10,18,1]{2,3,1,0:T(1,128)} %copy-done.18) | data formatting | bytes 7200 | tf_op jit(solution)/shard_map/ppermute | solution.py:26
  60.8 1.2 %copy.82 = f32[5,10,18,1]{3,2,0,1:T(8,128)} copy(f32[5,10,18,1]{2,3,1,0:T(1,128)S(1)} %copy-done.17) | data formatting | bytes 7200 | tf_op jit(solution)/shard_map/ppermute | solution.py:24
  62.0 0.5 copy.95
  62.5 1.2 %copy.96 = f32[5,12,20,1]{3,2,0,1:T(8,128)S(1)} copy(f32[5,12,20,1]{2,3,1,0:T(1,128)} %collective-permute-done.11) | data formatting | bytes 9600 | tf_op jit(solution)/shard_map/ppermute | solution.py:26
  63.7 1.9 %maximum_bitcast_fusion = f32[12,5,20,132]{3,2,1,0:T(8,128)S(1)} fusion(f32[5,12,20,1]{3,2,0,1:T(8,128)S(1)} %copy.96, f32[5,12,1,130]{3,2,0,1:T(1,128)} %copy-done.8, f32[5,1,18,130]{3,2,0,1:T(8,128)} %copy-done.5, f32[5,10,18,130]{3,2,0,1:T(8,128)S(1)} %add_bitcast_fusion, f32[5,1,18,130]{3,2,0,1:T(8,128)S(1)} %collective-permute-done.6, ...), kind=kLoop, calls=%fused_computation.86 | loop fusion | flops 950400 | bytes 1267200 | tf_op jit(solution)/shard_map/transpose | solution.py:136
  65.8 1.8 %scatter-add.24 = f32[16,5,8,132]{3,0,1,2:T(8,128)S(1)} dynamic-update-slice(f32[16,5,8,132]{3,0,1,2:T(8,128)S(1)} %slice.448, f32[1,5,8,132]{3,0,1,2:T(1,128)S(1)} %slice_add_fusion.5, s32[]{:T(128)} %constant.386.clone.1, s32[]{:T(128)} %constant.386.clone.1, s32[]{:T(128)} %constant.386.clone.1, s32[]{:T(128)} %constant.386.clone.1) | dynamic-update-slice | bytes 42244 | tf_op jit(solution)/shard_map/scatter-add | solution.py:137
  67.8 1.8 %scatter-add.25 = f32[16,5,8,132]{3,0,1,2:T(8,128)S(1)} dynamic-update-slice(f32[16,5,8,132]{3,0,1,2:T(8,128)S(1)} %scatter-add.24, f32[1,5,8,132]{3,0,1,2:T(1,128)S(1)} %slice_add_fusion.4, s32[]{:T(128)} %constant.390.clone.1, s32[]{:T(128)} %constant.386.clone.1, s32[]{:T(128)} %constant.386.clone.1, s32[]{:T(128)} %constant.386.clone.1) | dynamic-update-slice | bytes 42244 | tf_op jit(solution)/shard_map/scatter-add | solution.py:137
  70.0 2.8 %scatter-add.26 = f32[128,5,8,16]{0,3,1,2:T(8,128)S(1)} dynamic-update-slice(f32[128,5,8,16]{0,3,1,2:T(8,128)S(1)} %slice.453, f32[1,5,8,16]{0,3,1,2:T(8,128)S(1)} %slice_add_fusion.1, s32[]{:T(128)} %constant.386.clone.1, s32[]{:T(128)} %constant.386.clone.1, s32[]{:T(128)} %constant.386.clone.1, s32[]{:T(128)} %constant.386.clone.1) | dynamic-update-slice | bytes 5124 | tf_op jit(solution)/shard_map/scatter-add | solution.py:137
  73.0 5.3 %scatter-add.29 = f32[128,5,8,16]{0,3,1,2:T(8,128)S(1)} dynamic-update-slice(f32[128,5,8,16]{0,3,1,2:T(8,128)S(1)} %scatter-add.26, f32[1,5,8,16]{0,3,1,2:T(8,128)S(1)} %slice_add_fusion, s32[]{:T(128)} %constant.391.clone.1, s32[]{:T(128)} %constant.386.clone.1, s32[]{:T(128)} %constant.386.clone.1, s32[]{:T(128)} %constant.386.clone.1) | dynamic-update-slice | bytes 5124 | tf_op jit(solution)/shard_map/scatter-add | solution.py:137
  78.4 1.6 %fusion.36 = f32[5,8,16,128]{3,2,0,1:T(8,128)S(1)} fusion(f32[5,8,16,128]{3,2,0,1:T(8,128)S(1)} %copy-done.4, f32[128,5,8,16]{0,3,1,2:T(8,128)S(1)} %scatter-add.29, f32[5,8,16,128]{3,2,1,0:T(8,128)} %param.24, f32[5,10,1,128]{3,2,0,1:T(1,128)S(1)} %collective-permute-done.2, f32[5,10,16,128]{3,2,0,1:T(8,128)S(1)} %copy-done.1, ...), kind=kLoop, calls=%fused_computation.118 | loop fusion | flops 2785280 | bytes 2057248 | tf_op jit(solution)/shard_map/add | solution.py:130
  80.0 0.8 copy.98
  (140 shorter events, 8.5 us)
Async XLA Ops:
  0.8 4.1 %collective-permute-start.1 = (f32[5,1,16,128]{3,2,0,1:T(8,128)S(1)}, f32[5,1,16,128]{3,2,0,1:T(8,128)S(1)}, u32[]{:S(2)}, u32[]{:S(2)}) collective-permute-start(f32[5,1,16,128]{3,2,0,1:T(8,128)S(1)} %get-tuple-element.522), channel_id=1, source_target_pairs={{0,8},{8,16},{16,24},{24,0},{1,9},{9,17},{17,25},{25,1},{2,10},{10... | collective-permute-start | bytes 122888 | tf_op jit(solution)/shard_map/ppermute | solution.py:24
  1.3 4.6 %collective-permute-start = (f32[5,1,16,128]{3,2,0,1:T(8,128)S(1)}, f32[5,1,16,128]{3,2,0,1:T(8,128)S(1)}, u32[]{:S(2)}, u32[]{:S(2)}) collective-permute-start(f32[5,1,16,128]{3,2,0,1:T(8,128)S(1)} %get-tuple-element.521), channel_id=1, source_target_pairs={{8,0},{16,8},{24,16},{0,24},{9,1},{17,9},{25,17},{1,25},{10,2},{18... | collective-permute-start | bytes 122888 | tf_op jit(solution)/shard_map/ppermute | solution.py:26
  4.9 5.6 %copy-start.12 = (f32[5,1,16,128]{3,2,0,1:T(8,128)}, f32[5,1,16,128]{3,2,0,1:T(8,128)S(1)}, u32[]{:S(2)}) copy-start(f32[5,1,16,128]{3,2,0,1:T(8,128)S(1)} %collective-permute-done.1) | copy-start | bytes 122884
  6.0 4.5 %copy-start.14 = (f32[5,1,16,128]{3,2,0,1:T(8,128)}, f32[5,1,16,128]{3,2,0,1:T(8,128)S(1)}, u32[]{:S(2)}) copy-start(f32[5,1,16,128]{3,2,0,1:T(8,128)S(1)} %collective-permute-done) | copy-start | bytes 122884
  6.0 13.4 %copy-start = (f32[5,10,16,128]{3,2,0,1:T(8,128)}, f32[5,10,16,128]{3,2,0,1:T(8,128)S(1)}, u32[]{:S(2)}) copy-start(f32[5,10,16,128]{3,2,0,1:T(8,128)S(1)} %constant_dynamic-update-slice_fusion) | copy-start | bytes 1228804
  6.0 6.0 %collective-permute-start.2 = (f32[5,10,1,128]{3,2,0,1:T(1,128)S(1)}, f32[5,10,1,128]{3,2,0,1:T(1,128)S(1)}, u32[]{:S(2)}, u32[]{:S(2)}) collective-permute-start(f32[5,10,1,128]{3,2,0,1:T(1,128)S(1)} %get-tuple-element.517), channel_id=1, source_target_pairs={{2,0},{4,2},{6,4},{0,6},{3,1},{5,3},{7,5},{1,7},{10,8},{12,10},{14... | collective-permute-start | bytes 76808 | tf_op jit(solution)/shard_map/ppermute | solution.py:26
  10.5 5.6 %collective-permute-start.3 = (f32[5,10,1,128]{3,2,0,1:T(1,128)S(1)}, f32[5,10,1,128]{3,2,0,1:T(1,128)S(1)}, u32[]{:S(2)}, u32[]{:S(2)}) collective-permute-start(f32[5,10,1,128]{3,2,0,1:T(1,128)S(1)} %get-tuple-element.516), channel_id=1, source_target_pairs={{0,2},{2,4},{4,6},{6,0},{1,3},{3,5},{5,7},{7,1},{8,10},{10,12},{12... | collective-permute-start | bytes 76808 | tf_op jit(solution)/shard_map/ppermute | solution.py:24
  16.1 3.2 %copy-start.9 = (f32[5,10,1,128]{3,2,0,1:T(1,128)}, f32[5,10,1,128]{3,2,0,1:T(1,128)S(1)}, u32[]{:S(2)}) copy-start(f32[5,10,1,128]{3,2,0,1:T(1,128)S(1)} %collective-permute-done.3) | copy-start | bytes 76804
  16.8 4.0 %collective-permute-start.5 = (f32[5,10,18,1]{2,3,1,0:T(1,128)S(1)}, f32[5,10,18,1]{2,3,1,0:T(1,128)S(1)}, u32[]{:S(2)}, u32[]{:S(2)}) collective-permute-start(f32[5,10,18,1]{2,3,1,0:T(1,128)S(1)} %copy.81), channel_id=1, source_target_pairs={{0,1},{1,0},{2,3},{3,2},{4,5},{5,4},{6,7},{7,6},{8,9},{9,8},{10,11... | collective-permute-start | bytes 10808 | tf_op jit(solution)/shard_map/ppermute | solution.py:24
  18.8 3.9 %collective-permute-start.4 = (f32[5,10,18,1]{2,3,1,0:T(1,128)S(1)}, f32[5,10,18,1]{2,3,1,0:T(1,128)S(1)}, u32[]{:S(2)}, u32[]{:S(2)}) collective-permute-start(f32[5,10,18,1]{2,3,1,0:T(1,128)S(1)} %copy.79), channel_id=1, source_target_pairs={{1,0},{0,1},{3,2},{2,3},{5,4},{4,5},{7,6},{6,7},{9,8},{8,9},{11,10... | collective-permute-start | bytes 10808 | tf_op jit(solution)/shard_map/ppermute | solution.py:26
  20.8 2.7 %copy-start.16 = (f32[5,10,18,1]{2,3,1,0:T(1,128)}, f32[5,10,18,1]{2,3,1,0:T(1,128)S(1)}, u32[]{:S(2)}) copy-start(f32[5,10,18,1]{2,3,1,0:T(1,128)S(1)} %collective-permute-done.5) | copy-start | bytes 10804
  22.7 0.9 %copy-start.18 = (f32[5,10,18,1]{2,3,1,0:T(1,128)}, f32[5,10,18,1]{2,3,1,0:T(1,128)S(1)}, u32[]{:S(2)}) copy-start(f32[5,10,18,1]{2,3,1,0:T(1,128)S(1)} %collective-permute-done.4) | copy-start | bytes 10804
  24.1 1.2 %copy-start.6 = (f32[1,1,1,3,16,128]{5,4,3,2,1,0:T(8,128)S(1)}, f32[1,1,1,3,16,128]{5,4,3,2,1,0:T(8,128)}, u32[]{:S(2)}) copy-start(f32[1,1,1,3,16,128]{5,4,3,2,1,0:T(8,128)} %param.28) | copy-start | bytes 73732
  24.1 1.2 %copy-start.11 = (s32[1,1,1,16,128]{4,3,2,1,0:T(8,128)S(1)}, s32[1,1,1,16,128]{4,3,2,1,0:T(8,128)}, u32[]{:S(2)}) copy-start(s32[1,1,1,16,128]{4,3,2,1,0:T(8,128)} %param.25) | copy-start | bytes 24580
  24.1 1.2 %copy-start.15 = (f32[1,1,1,3,16,128]{5,4,3,2,1,0:T(8,128)S(1)}, f32[1,1,1,3,16,128]{5,4,3,2,1,0:T(8,128)}, u32[]{:S(2)}) copy-start(f32[1,1,1,3,16,128]{5,4,3,2,1,0:T(8,128)} %param.29) | copy-start | bytes 73732
  24.1 1.2 %copy-start.19 = (f32[1,1,1,16,128]{4,3,2,1,0:T(8,128)S(1)}, f32[1,1,1,16,128]{4,3,2,1,0:T(8,128)}, u32[]{:S(2)}) copy-start(f32[1,1,1,16,128]{4,3,2,1,0:T(8,128)} %param.30) | copy-start | bytes 24580
  24.1 1.2 %copy-start.20 = (f32[1,1,1,16,128]{4,3,2,1,0:T(8,128)S(1)}, f32[1,1,1,16,128]{4,3,2,1,0:T(8,128)}, u32[]{:S(2)}) copy-start(f32[1,1,1,16,128]{4,3,2,1,0:T(8,128)} %param.31) | copy-start | bytes 24580
  24.1 1.2 %copy-start.21 = (s32[1,1,1,16]{3,2,1,0:T(1,128)S(1)}, s32[1,1,1,16]{3,2,1,0:T(1,128)}, u32[]{:S(2)}) copy-start(s32[1,1,1,16]{3,2,1,0:T(1,128)} %param.26) | copy-start | bytes 196
  24.2 1.2 %copy-start.22 = (s32[1,1,1,16]{3,2,1,0:T(1,128)S(1)}, s32[1,1,1,16]{3,2,1,0:T(1,128)}, u32[]{:S(2)}) copy-start(s32[1,1,1,16]{3,2,1,0:T(1,128)} %param.27) | copy-start | bytes 196
  41.3 4.4 %collective-permute-start.6 = (f32[5,1,18,130]{3,2,0,1:T(8,128)S(1)}, f32[5,1,18,130]{3,2,0,1:T(8,128)S(1)}, u32[]{:S(2)}, u32[]{:S(2)}) collective-permute-start(f32[5,1,18,130]{3,2,0,1:T(8,128)S(1)} %get-tuple-element.512), channel_id=1, source_target_pairs={{0,8},{8,16},{16,24},{24,0},{1,9},{9,17},{17,25},{25,1},{2,10},{10... | collective-permute-start | bytes 140408 | tf_op jit(solution)/shard_map/ppermute | solution.py:24
  41.3 4.6 %collective-permute-start.7 = (f32[5,1,18,130]{3,2,0,1:T(8,128)S(1)}, f32[5,1,18,130]{3,2,0,1:T(8,128)S(1)}, u32[]{:S(2)}, u32[]{:S(2)}) collective-permute-start(f32[5,1,18,130]{3,2,0,1:T(8,128)S(1)} %get-tuple-element.513), channel_id=1, source_target_pairs={{8,0},{16,8},{24,16},{0,24},{9,1},{17,9},{25,17},{1,25},{10,2},{18... | collective-permute-start | bytes 140408 | tf_op jit(solution)/shard_map/ppermute | solution.py:26
  46.0 6.6 %copy-start.5 = (f32[5,1,18,130]{3,2,0,1:T(8,128)}, f32[5,1,18,130]{3,2,0,1:T(8,128)S(1)}, u32[]{:S(2)}) copy-start(f32[5,1,18,130]{3,2,0,1:T(8,128)S(1)} %collective-permute-done.7) | copy-start | bytes 140404
  46.1 6.5 %collective-permute-start.8 = (f32[5,12,1,130]{3,2,0,1:T(1,128)S(1)}, f32[5,12,1,130]{3,2,0,1:T(1,128)}, u32[]{:S(2)}, u32[]{:S(2)}) collective-permute-start(f32[5,12,1,130]{3,2,0,1:T(1,128)S(1)} %get-tuple-element.510), channel_id=1, source_target_pairs={{0,2},{2,4},{4,6},{6,0},{1,3},{3,5},{5,7},{7,1},{8,10},{10,12},{12... | collective-permute-start | bytes 93608 | tf_op jit(solution)/shard_map/ppermute | solution.py:24
  46.2 6.5 %collective-permute-start.9 = (f32[5,12,1,130]{3,2,0,1:T(1,128)S(1)}, f32[5,12,1,130]{3,2,0,1:T(1,128)S(1)}, u32[]{:S(2)}, u32[]{:S(2)}) collective-permute-start(f32[5,12,1,130]{3,2,0,1:T(1,128)S(1)} %get-tuple-element.511), channel_id=1, source_target_pairs={{2,0},{4,2},{6,4},{0,6},{3,1},{5,3},{7,5},{1,7},{10,8},{12,10},{14... | collective-permute-start | bytes 93608 | tf_op jit(solution)/shard_map/ppermute | solution.py:26
  52.6 0.6 copy-start.8
  54.6 3.6 %copy-start.2 = (f32[5,8,16,128]{3,2,1,0:T(8,128)S(1)}, f32[5,8,16,128]{3,2,1,0:T(8,128)}, u32[]{:S(2)}) copy-start(f32[5,8,16,128]{3,2,1,0:T(8,128)} %param.23) | copy-start | bytes 983044
  55.7 5.1 %copy-start.17 = (f32[5,10,18,1]{2,3,1,0:T(1,128)S(1)}, f32[5,10,18,1]{2,3,1,0:T(1,128)}, u32[]{:S(2)}) copy-start(f32[5,10,18,1]{2,3,1,0:T(1,128)} %copy-done.16) | copy-start | bytes 10804
  55.7 6.3 %collective-permute-start.10 = (f32[5,12,20,1]{2,3,1,0:T(1,128)}, f32[5,12,20,1]{2,3,1,0:T(1,128)S(1)}, u32[]{:S(2)}, u32[]{:S(2)}) collective-permute-start(f32[5,12,20,1]{2,3,1,0:T(1,128)} %copy.93), channel_id=1, source_target_pairs={{0,1},{1,0},{2,3},{3,2},{4,5},{5,4},{6,7},{7,6},{8,9},{9,8},{10,11... | collective-permute-start | bytes 14408 | tf_op jit(solution)/shard_map/ppermute | solution.py:24
  56.7 5.8 %collective-permute-start.11 = (f32[5,12,20,1]{2,3,1,0:T(1,128)S(1)}, f32[5,12,20,1]{2,3,1,0:T(1,128)}, u32[]{:S(2)}, u32[]{:S(2)}) collective-permute-start(f32[5,12,20,1]{2,3,1,0:T(1,128)S(1)} %copy.94), channel_id=1, source_target_pairs={{1,0},{0,1},{3,2},{2,3},{5,4},{4,5},{7,6},{6,7},{9,8},{8,9},{11,10... | collective-permute-start | bytes 14408 | tf_op jit(solution)/shard_map/ppermute | solution.py:26
  69.8 8.6 %copy-start.1 = (f32[5,10,16,128]{3,2,0,1:T(8,128)S(1)}, f32[5,10,16,128]{3,2,0,1:T(8,128)}, u32[]{:S(2)}) copy-start(f32[5,10,16,128]{3,2,0,1:T(8,128)} %copy-done) | copy-start | bytes 1228804
  69.8 8.6 %copy-start.3 = (f32[5,10,18,1]{3,2,0,1:T(8,128)S(1)}, f32[5,10,18,1]{3,2,0,1:T(8,128)}, u32[]{:S(2)}) copy-start(f32[5,10,18,1]{3,2,0,1:T(8,128)} %copy.82) | copy-start | bytes 10804
  69.8 8.6 %copy-start.4 = (f32[5,8,16,128]{3,2,0,1:T(8,128)S(1)}, f32[5,8,16,128]{3,2,0,1:T(8,128)}, u32[]{:S(2)}) copy-start(f32[5,8,16,128]{3,2,0,1:T(8,128)} %copy.97) | copy-start | bytes 983044
  69.8 8.6 %copy-start.7 = (f32[8,16,128]{2,1,0:T(8,128)S(1)}, f32[8,16,128]{2,1,0:T(8,128)}, u32[]{:S(2)}) copy-start(f32[8,16,128]{2,1,0:T(8,128)} %get-tuple-element.519) | copy-start | bytes 196612
  69.8 8.6 %copy-start.10 = (f32[5,10,1,128]{3,2,0,1:T(1,128)S(1)}, f32[5,10,1,128]{3,2,0,1:T(1,128)}, u32[]{:S(2)}) copy-start(f32[5,10,1,128]{3,2,0,1:T(1,128)} %copy-done.9) | copy-start | bytes 76804
  69.8 8.6 %copy-start.13 = (f32[5,1,16,128]{3,2,0,1:T(8,128)S(1)}, f32[5,1,16,128]{3,2,0,1:T(8,128)}, u32[]{:S(2)}) copy-start(f32[5,1,16,128]{3,2,0,1:T(8,128)} %copy-done.12) | copy-start | bytes 122884
where the time goes:
time: 81.1 us; the launch traced here: 80.7 us
  local copies, waits for them, and re-layouts  30.3 us (37%)
  starting transfers between devices  16.8 us (21%)
  waiting for transfers between devices  15.6 us (19%)
  other arithmetic  8.65 us (11%)
  matrix products  8.55 us (11%)
    ppermute x6, starting transfers between devices, with_halo(): lax.ppermute(head, axis, [((i + 1) % count, i) for i in range(count)])  14.1 us
    ppermute x6, waiting for transfers between devices, with_halo(): lax.ppermute(tail, axis, [(i, (i + 1) % count) for i in range(count)])  12.3 us
    scatter-add x4, local copies, waits for them, and re-layouts, fold_rim(): moved_axis[2:-2].at[0].add(moved_axis[0]).at[-1].add(moved_axis[-1])  11.8 us
    dot_general x2, matrix products, deposit_group(): jnp.einsum('bt,bkz->tkz', owners, spread_sources, precision=lax.Precision...  5.33 us
    ppermute x6, waiting for transfers between devices, with_halo(): lax.ppermute(head, axis, [((i + 1) % count, i) for i in range(count)])  3.25 us
    unnamed x52, local copies, waits for them, and re-layouts  2.73 us
    ppermute x6, starting transfers between devices, with_halo(): lax.ppermute(tail, axis, [(i, (i + 1) % count) for i in range(count)])  2.7 us
    ppermute x3, local copies, waits for them, and re-layouts, with_halo(): lax.ppermute(head, axis, [((i + 1) % count, i) for i in range(count)])  2.39 us
  transfers between devices with their start and end apart: 12, of which 8 were waited for; matrix products, arithmetic and copies ran while one was open for 8% of the time, Pallas kernels for 0%

commit v1 on v0

v1 whole, which is shorter than its diff:
```python
import functools

import jax
import jax.numpy as jnp
from jax import lax
from jax.experimental import pallas as pl
from jax.experimental.pallas import tpu as pltpu
from jax.sharding import PartitionSpec as P

TS = 8
PARCEL = 8.0
LATENT = 0.5
TIME_INCREMENT = 0.2
VISCOSITY = 0.5
MESH = pl.DeviceIdType.MESH
LANES = 128
F32 = jnp.float32
BF16 = jnp.bfloat16

DIRS = ((-1, 0), (1, 0), (0, -1), (0, 1), (-1, -1), (-1, 1), (1, -1), (1, 1))
OPPOSITE = (1, 0, 3, 2, 7, 6, 5, 4)


def int_div(values, number):
    if number & (number - 1) == 0:
        return lax.shift_right_logical(values, jnp.int32(number.bit_length() - 1))
    return lax.div(values, jnp.int32(number))


def int_mod(values, number):
    if number & (number - 1) == 0:
        return values & jnp.int32(number - 1)
    return lax.rem(values, jnp.int32(number))


def tap(places, anchor, low, middle, high):
    return jnp.where(
        places == anchor,
        low,
        jnp.where(places == anchor + 1, middle, jnp.where(places == anchor + 2, high, 0.0)),
    )


def kernel(
    tile_ref,
    count_ref,
    gas_ref,
    cell_ref,
    frac_ref,
    vel_ref,
    mass_ref,
    temp_ref,
    out_ref,
    weight_ref,
    planar_ref,
    vert_ref,
    vghost_ref,
    scaled_ref,
    sghost_ref,
    lhs_ref,
    ghost_ref,
    ysend_ref,
    csend_ref,
    crecv_ref,
    zsend_ref,
    zrecv_ref,
    gasat_ref,
    source_ref,
    dep_ref,
    dcsend_ref,
    dzsend_ref,
    dzrecv_ref,
    dxrecv_ref,
    dyrecv_ref,
    dcrecv_ref,
    send_sem,
    recv_sem,
):
    comps, cx, cy, cz = gas_ref.shape
    blocks, slots = cell_ref.shape
    plane = cx * cy
    starts = (0, cy, 2 * cy, 2 * cy + cx)
    sizes = (cy, cy, cx, cx)
    corner_at = 2 * cy + 2 * cx
    width = lhs_ref.shape[1]
    used = dep_ref.shape[1]

    ix, iy, iz = lax.axis_index("gx"), lax.axis_index("gy"), lax.axis_index("gz")
    nx, ny, nz = lax.axis_size("gx"), lax.axis_size("gy"), lax.axis_size("gz")

    def xy_id(k):
        dx, dy = DIRS[k]
        return {"gx": lax.rem(ix + dx + nx, nx), "gy": lax.rem(iy + dy + ny, ny), "gz": iz}

    def z_id(side):
        return {"gx": ix, "gy": iy, "gz": lax.rem(iz + (2 * side - 1) + nz, nz)}

    barrier = pltpu.get_barrier_semaphore()
    for k in range(8):
        pl.semaphore_signal(barrier, inc=1, device_id=xy_id(k), device_id_type=MESH)
    for side in range(2):
        pl.semaphore_signal(barrier, inc=1, device_id=z_id(side), device_id_type=MESH)

    csend_ref[...] = jnp.zeros_like(csend_ref)
    zsend_ref[...] = jnp.zeros_like(zsend_ref)
    ghost_ref[:, corner_at:, :] = jnp.zeros(
        (comps, ghost_ref.shape[1] - corner_at, cz), F32
    )
    ysend_ref[0] = gas_ref[:, :, 0, :]
    ysend_ref[1] = gas_ref[:, :, cy - 1, :]
    for j in range(4):
        dx, dy = DIRS[4 + j]
        csend_ref[j, :comps, :] = gas_ref[:, 0 if dx < 0 else cx - 1, 0 if dy < 0 else cy - 1, :]

    pl.semaphore_wait(barrier, 10)

    def xy_copy(k, base, src, dst):
        return pltpu.make_async_remote_copy(
            src_ref=src,
            dst_ref=dst,
            send_sem=send_sem.at[base + k],
            recv_sem=recv_sem.at[base + OPPOSITE[k]],
            device_id=xy_id(k),
            device_id_type=MESH,
        )

    halo = []
    for k in (4, 5, 6, 7, 0, 1, 2, 3):
        other = OPPOSITE[k]
        if k < 2:
            src = gas_ref.at[:, 0 if k == 0 else cx - 1]
        elif k < 4:
            src = ysend_ref.at[k - 2]
        else:
            src = csend_ref.at[k - 4]
        if k < 4:
            dst = ghost_ref.at[:, pl.ds(starts[other], sizes[other])]
        else:
            dst = crecv_ref.at[other - 4]
        copy = xy_copy(k, 0, src, dst)
        copy.start()
        halo.append(copy)

    cells = cell_ref[...]
    weight_ref[0] = int_div(cells, TS * cz).astype(F32)
    weight_ref[1] = int_mod(int_div(cells, cz), TS).astype(F32)
    weight_ref[2] = int_mod(cells, cz).astype(F32)
    for axis in range(3):
        offset = frac_ref[axis]
        weight_ref[3 + 3 * axis] = 0.5 * (0.5 - offset) * (0.5 - offset)
        weight_ref[4 + 3 * axis] = 0.75 - offset * offset
        weight_ref[5 + 3 * axis] = 0.5 * (0.5 + offset) * (0.5 + offset)

    tiles_y = cy // TS

    def lane_block(b):
        return pl.ds(pl.multiple_of(b * slots, slots), slots)

    def places(rows, first):
        return (lax.broadcasted_iota(jnp.int32, (rows, slots), 0) + first).astype(F32)

    def ends(length):
        row = lax.broadcasted_iota(jnp.int32, (8, slots), 0)
        return jnp.where(row == 0, 0, jnp.where(row == 1, length + 1, -8)).astype(F32)

    def make_weights(b, carry):
        def row(i):
            return weight_ref[i, pl.ds(b, 1), :]

        tile = tile_ref[b]
        corner_x = (int_div(tile, tiles_y) * TS).astype(F32)
        corner_y = (int_mod(tile, tiles_y) * TS).astype(F32)
        anchor_x, anchor_y, anchor_z = row(0) + corner_x, row(1) + corner_y, row(2)
        tx, ty, tz = [tuple(row(3 + 3 * a + i) for i in range(3)) for a in range(3)]
        wx, wxe = tap(places(cx, 1), anchor_x, *tx), tap(ends(cx), anchor_x, *tx)
        wy, wye = tap(places(cy, 1), anchor_y, *ty), tap(ends(cy), anchor_y, *ty)
        corners = [
            wxe[0 if dx < 0 else 1][None] * wye[0 if dy < 0 else 1][None] for dx, dy in DIRS[4:]
        ]
        planar = jnp.concatenate(
            [
                (wx[:, None, :] * wy[None, :, :]).reshape(plane, slots),
                wxe[0:1] * wy,
                wxe[1:2] * wy,
                wx * wye[0:1],
                wx * wye[1:2],
            ]
            + corners
            + [jnp.zeros((width - plane - corner_at - 4, slots), F32)],
            axis=0,
        )
        at = lane_block(b)
        planar_ref[:, at] = planar.astype(BF16)
        vert_ref[:, at] = tap(places(cz, 1), anchor_z, *tz).astype(BF16)
        vghost_ref[b] = tap(ends(cz), anchor_z, *tz).astype(BF16).astype(F32)
        return carry

    lax.fori_loop(0, blocks, make_weights, 0)

    for c in range(comps):
        turned = gas_ref[c].reshape(plane, cz).T
        lhs_ref[c * cz : (c + 1) * cz, :plane] = turned.astype(BF16)
        zsend_ref[0, c : c + 1, :plane] = turned[0:1]
        zsend_ref[1, c : c + 1, :plane] = turned[cz - 1 : cz]

    for copy in halo:
        copy.wait_recv()

    for c in range(comps):
        ghost_ref[c, corner_at : corner_at + 4, :] = crecv_ref[:, c, :]
        turned = ghost_ref[c].T
        lhs_ref[c * cz : (c + 1) * cz, plane:] = turned.astype(BF16)
        zsend_ref[0, c : c + 1, plane:] = turned[0:1]
        zsend_ref[1, c : c + 1, plane:] = turned[cz - 1 : cz]

    def z_copy(side, base, src, dst):
        return pltpu.make_async_remote_copy(
            src_ref=src.at[side],
            dst_ref=dst.at[1 - side],
            send_sem=send_sem.at[base + side],
            recv_sem=recv_sem.at[base + 1 - side],
            device_id=z_id(side),
            device_id_type=MESH,
        )

    z_halo = [z_copy(side, 8, zsend_ref, zrecv_ref) for side in range(2)]
    for copy in z_halo:
        copy.start()

    pair = 2 if blocks % 2 == 0 else 1

    def gather(i, carry):
        at = pl.ds(pl.multiple_of(i * pair * slots, pair * slots), pair * slots)
        planar = planar_ref[:, at]
        vertical = vert_ref[:, at].astype(F32)
        for c in range(comps):
            near = jnp.dot(
                lhs_ref[c * cz : (c + 1) * cz, :], planar, preferred_element_type=F32
            )
            value = jnp.sum(near * vertical, axis=0, keepdims=True)
            for j in range(pair):
                gasat_ref[c, pl.ds(i * pair + j, 1), :] = value[:, j * slots : (j + 1) * slots]
        return carry

    lax.fori_loop(0, blocks // pair, gather, 0)

    for copy in z_halo:
        copy.wait_recv()

    z_values = jnp.concatenate([zrecv_ref[0], zrecv_ref[1]], axis=0).astype(BF16)
    near_ends = jnp.dot(z_values, planar_ref[...], preferred_element_type=F32)
    for b in range(blocks):
        part = near_ends[:, b * slots : (b + 1) * slots]
        both = part[:8] * vghost_ref[b, 0:1, :] + part[8:] * vghost_ref[b, 1:2, :]
        for c in range(comps):
            gasat_ref[c, b : b + 1, :] += both[c : c + 1]

    temper = temp_ref[...]
    diameter = jnp.exp(jnp.log(mass_ref[...]) * (1.0 / 3.0))
    excess = gasat_ref[4] - temper
    spalding = jnp.maximum(excess, 0.0) + jnp.log1p(jnp.exp(-jnp.abs(excess)))
    rate = diameter * jnp.log1p(spalding)
    drag = diameter * gasat_ref[0]
    heat = diameter * excess
    source_ref[0] = rate
    for a in range(3):
        velocity = vel_ref[a]
        source_ref[1 + a] = rate * velocity - drag * (gasat_ref[1 + a] - velocity)
    source_ref[4] = -heat - LATENT * rate

    sghost_ref[...] = jnp.zeros_like(sghost_ref)
    slot_ids = lax.broadcasted_iota(jnp.int32, (1, slots), 1)

    def scale(b, carry):
        at = lane_block(b)
        alive = jnp.where(slot_ids < count_ref[b], PARCEL, 0.0)
        vertical = vert_ref[:, at].astype(F32)
        low, high = vghost_ref[b, 0:1, :], vghost_ref[b, 1:2, :]
        rows = []
        for c in range(comps):
            strength = source_ref[c, pl.ds(b, 1), :] * alive
            scaled_ref[c * cz : (c + 1) * cz, at] = (vertical * strength).astype(BF16)
            rows.append(strength)
        strengths = jnp.concatenate(rows + [jnp.zeros((8 - comps, slots), F32)], axis=0)
        sghost_ref[:, at] = jnp.concatenate([strengths * low, strengths * high], axis=0).astype(BF16)
        return carry

    lax.fori_loop(0, blocks, scale, 0)

    def contract(lhs, rhs):
        return lax.dot_general(lhs, rhs, (((1,), (1,)), ((), ())), preferred_element_type=F32)

    z_ends = contract(sghost_ref[...], planar_ref[...])
    dzsend_ref[0] = z_ends[:8]
    dzsend_ref[1] = z_ends[8:]
    z_deposit = [z_copy(side, 10, dzsend_ref, dzrecv_ref) for side in range(2)]
    for copy in z_deposit:
        copy.start()

    for c in range(comps):
        dep_ref[c] = contract(planar_ref[:used, :], scaled_ref[c * cz : (c + 1) * cz, :])

    for copy in z_deposit:
        copy.wait_recv()

    lane = lax.broadcasted_iota(jnp.int32, (plane, cz), 1)
    row_y = int_mod(lax.broadcasted_iota(jnp.int32, (plane, cz), 0), cy)

    def columns(ref, first):
        both = jnp.concatenate([ref[0], ref[1]], axis=0)[:, first : first + LANES]
        return jnp.concatenate([both, jnp.zeros((LANES - 16, LANES), F32)], axis=0).T

    def at_ends(turned, rows, c):
        lanes = lax.broadcasted_iota(jnp.int32, (rows, cz), 1)
        low, high = turned[:rows, c : c + 1], turned[:rows, 8 + c : 9 + c]
        return jnp.where(lanes == 0, low, 0.0) + jnp.where(lanes == cz - 1, high, 0.0)

    outer = columns(dzrecv_ref, plane)
    dcsend_ref[...] = jnp.zeros_like(dcsend_ref)
    for c in range(comps):
        dep_ref[c, plane:, :] += at_ends(outer, used - plane, c)
        for j in range(4):
            dcsend_ref[j, c : c + 1, :] = dep_ref[c, plane + corner_at + j : plane + corner_at + j + 1, :]

    deposit = []
    for k in (4, 5, 6, 7, 0, 1, 2, 3):
        other = OPPOSITE[k]
        if k < 4:
            src = dep_ref.at[:, pl.ds(plane + starts[k], sizes[k])]
            dst = (dxrecv_ref if k < 2 else dyrecv_ref).at[other % 2]
        else:
            src, dst = dcsend_ref.at[k - 4], dcrecv_ref.at[other - 4]
        copy = xy_copy(k, 12, src, dst)
        copy.start()
        deposit.append(copy)

    inner = columns(dzrecv_ref, 0)
    z_sides = columns(zrecv_ref, 0)
    flow = [gas_ref[1 + a].reshape(plane, cz) for a in range(3)]
    for c in range(comps):
        cube = gas_ref[c]
        q = cube.reshape(plane, cz)
        x_low = jnp.concatenate([ghost_ref[c, 0:cy], q[: plane - cy]], axis=0)
        x_high = jnp.concatenate([q[cy:], ghost_ref[c, cy : 2 * cy]], axis=0)

        def edge(first):
            ghost = ghost_ref[c, first : first + cx]
            return jnp.broadcast_to(ghost[:, None, :], (cx, cy, cz)).reshape(plane, cz)

        y_low = jnp.where(row_y == 0, edge(2 * cy), pltpu.roll(q, 1, 0))
        y_high = jnp.where(row_y == cy - 1, edge(2 * cy + cx), pltpu.roll(q, plane - 1, 0))
        z_low = jnp.where(lane == 0, z_sides[:, c : c + 1], pltpu.roll(q, 1, 1))
        z_high = jnp.where(lane == cz - 1, z_sides[:, 8 + c : 9 + c], pltpu.roll(q, cz - 1, 1))
        laplace = -6.0 * q + x_high + x_low + y_high + y_low + z_high + z_low
        advect = 0.5 * (
            flow[0] * (x_high - x_low) + flow[1] * (y_high - y_low) + flow[2] * (z_high - z_low)
        )
        own = dep_ref[c, :plane, :] + at_ends(inner, plane, c)
        out_ref[c] = (q + TIME_INCREMENT * (VISCOSITY * laplace - advect + own)).reshape(cx, cy, cz)

    for copy in deposit:
        copy.wait_recv()

    for c in range(comps):
        for side in range(2):
            x_at, y_at = (cx - 1) * side, (cy - 1) * side
            out_ref[c, x_at] += TIME_INCREMENT * dxrecv_ref[side, c]
            out_ref[c, :, y_at, :] += TIME_INCREMENT * dyrecv_ref[side, c]
        for j in range(4):
            dx, dy = DIRS[4 + j]
            x_at, y_at = 0 if dx < 0 else cx - 1, 0 if dy < 0 else cy - 1
            out_ref[c, x_at, y_at : y_at + 1, :] += TIME_INCREMENT * dcrecv_ref[j, c : c + 1, :]

    for copy in halo + z_halo + z_deposit + deposit:
        copy.wait_send()


def local(
    gas_state,
    section_start,
    drop_cell,
    block_tile,
    droplets_per_block,
    drop_frac,
    drop_vel,
    drop_mass,
    drop_temp,
):
    comps, cx, cy, cz = gas_state.shape
    blocks, slots = drop_cell.shape[3:]
    plane = cx * cy
    ghosts = 2 * cx + 2 * cy + 4
    ghost_width = -(-ghosts // LANES) * LANES
    width = plane + ghost_width
    used = plane + -(-ghosts // 16) * 16
    total = blocks * slots
    smem = pl.BlockSpec(memory_space=pltpu.SMEM)
    vmem = pl.BlockSpec(memory_space=pltpu.VMEM)
    section = pl.pallas_call(
        kernel,
        out_shape=jax.ShapeDtypeStruct(gas_state.shape, F32),
        in_specs=[smem] * 2 + [vmem] * 6,
        out_specs=vmem,
        scratch_shapes=[
            pltpu.VMEM((12, blocks, slots), F32),
            pltpu.VMEM((width, total), BF16),
            pltpu.VMEM((cz, total), BF16),
            pltpu.VMEM((blocks, 8, slots), F32),
            pltpu.VMEM((comps * cz, total), BF16),
            pltpu.VMEM((16, total), BF16),
            pltpu.VMEM((comps * cz, width), BF16),
            pltpu.VMEM((comps, ghost_width, cz), F32),
            pltpu.VMEM((2, comps, cx, cz), F32),
            pltpu.VMEM((4, 8, cz), F32),
            pltpu.VMEM((4, 8, cz), F32),
            pltpu.VMEM((2, 8, width), F32),
            pltpu.VMEM((2, 8, width), F32),
            pltpu.VMEM((comps, blocks, slots), F32),
            pltpu.VMEM((comps, blocks, slots), F32),
            pltpu.VMEM((comps, used, cz), F32),
            pltpu.VMEM((4, 8, cz), F32),
            pltpu.VMEM((2, 8, width), F32),
            pltpu.VMEM((2, 8, width), F32),
            pltpu.VMEM((2, comps, cy, cz), F32),
            pltpu.VMEM((2, comps, cx, cz), F32),
            pltpu.VMEM((4, 8, cz), F32),
            pltpu.SemaphoreType.DMA((20,)),
            pltpu.SemaphoreType.DMA((20,)),
        ],
        compiler_params=pltpu.CompilerParams(collective_id=0, has_side_effects=True),
    )(
        block_tile.reshape(block_tile.shape[3:]),
        droplets_per_block.reshape(droplets_per_block.shape[3:]),
        gas_state,
        drop_cell.reshape(drop_cell.shape[3:]),
        drop_frac.reshape(drop_frac.shape[3:]),
        drop_vel.reshape(drop_vel.shape[3:]),
        drop_mass.reshape(drop_mass.shape[3:]),
        drop_temp.reshape(drop_temp.shape[3:]),
    )
    return 0.75 * section_start + 0.25 * section


def solution(mesh):
    in_specs = (
        P(None, "gx", "gy", "gz"),
        P(None, "gx", "gy", "gz"),
        P("gx", "gy", "gz", None, None),
        P("gx", "gy", "gz", None),
        P("gx", "gy", "gz", None),
        P("gx", "gy", "gz", None, None, None),
        P("gx", "gy", "gz", None, None, None),
        P("gx", "gy", "gz", None, None),
        P("gx", "gy", "gz", None, None),
    )
    out_specs = P(None, "gx", "gy", "gz")
    return jax.shard_map(local, mesh=mesh, in_specs=in_specs, out_specs=out_specs, check_vma=False)
```

time: 81.1 us -> 25.6 us (0.32)
  local copies, waits for them, and re-layouts: 30.3 us -> 0.01 us
  Pallas kernels: 0 us -> 23.7 us
  starting transfers between devices: 16.8 us -> 0 us
  waiting for transfers between devices: 15.6 us -> 0 us
  matrix products: 8.55 us -> 0 us
  other arithmetic: 8.65 us -> 1.74 us
    pallas_call x0 -> x1, Pallas kernels: none -> 23.7 us  [local(): pl.pallas_call(kernel, out_shape=jax.ShapeDtypeStruct(gas_state.shape, F3...]
    ppermute x12 -> x0, starting transfers between devices: 16.8 us -> none  [the longest x6 14.1 us: with_halo(): lax.ppermute(head, axis, [((i + 1) % count, i) for i in range(count)])]
    ppermute x12 -> x0, waiting for transfers between devices: 15.6 us -> none  [the longest x6 12.3 us: with_halo(): lax.ppermute(tail, axis, [(i, (i + 1) % count) for i in range(count)])]
    scatter-add x4 -> x0, local copies, waits for them, and re-layouts: 11.8 us -> none  [fold_rim(): moved_axis[2:-2].at[0].add(moved_axis[0]).at[-1].add(moved_axis[-1])]
    dot_general x6 -> x0, matrix products: 8.55 us -> none  [the longest x2 5.33 us: deposit_group(): jnp.einsum('bt,bkz->tkz', owners, spread_sources, precision=lax.Precision...]
    slice x20 -> x0, local copies, waits for them, and re-layouts: 4.58 us -> none  [the longest x6 1.98 us: with_halo(): lax.slice_in_dim(cells, cells.shape[dim] - width, cells.shape[dim], axis=...]
    ppermute x6 -> x0, local copies, waits for them, and re-layouts: 4.12 us -> none  [the longest x3 2.39 us: with_halo(): lax.ppermute(head, axis, [((i + 1) % count, i) for i in range(count)])]
    transpose x5 -> x0, other arithmetic: 2.91 us -> none  [the longest x1 1.85 us: fold_rim(): moved_axis = jnp.moveaxis(values, dim_index, 0)]
  transfers between devices with their start and end apart: 12 -> 0, of which waited for: 8 -> 0; matrix products, arithmetic and copies ran while one was open for 8% -> 0% of each run, Pallas kernels for 0% -> 0%
where the time goes in v1:
time: 25.6 us; the launch traced here: 25.5 us
  Pallas kernels  23.7 us (93%)
  other arithmetic  1.74 us (7%)
    pallas_call x1, Pallas kernels, local(): pl.pallas_call(kernel, out_shape=jax.ShapeDtypeStruct(gas_state.shape, F3...  23.7 us
    add x1, other arithmetic, local(): return 0.75 * section_start + 0.25 * section  1.74 us

profile of v1, /device:TPU:0, one launch (start us, length us, event | category | flops | bytes accessed | tf_op | source)
XLA Modules:
  0.0 25.5 jit_solution(8253599079198991957)
XLA Ops:
  0.0 0.0 copy-start
  0.0 23.7 %shard_map.91 = f32[5,8,16,128]{3,2,1,0:T(8,128)} custom-call(s32[16]{0:T(128)} %bitcast.12, s32[16]{0:T(128)} %bitcast.13, f32[5,8,16,128]{3,2,1,0:T(8,128)} %gas_ref.1, s32[16,128]{1,0:T(8,128)} %bitcast.9, f32[3,16,128]{2,1,0:T(8,128)} %bitcast.7, f32[3,16,128]{2,1,0:T(8,128)} %bitcast.8, f32[16,128]{1,0:T(8,128)} %bitcast.10, f32[16,128]{1,0:T(8,128)} %bitcast.11), custom_call_target="tpu_custom_call" | custom-call | tf_op jit(solution)/shard_map/pallas_call | solution.py:399
  23.7 0.0 copy-done
  23.7 1.7 %multiply_add_fusion = f32[5,8,16,128]{3,2,1,0:T(8,128)} fusion(f32[5,8,16,128]{3,2,1,0:T(8,128)} %shard_map.91, f32[5,8,16,128]{3,2,1,0:T(8,128)S(1)} %copy-done), kind=kLoop, calls=%fused_computation | loop fusion | flops 245760 | bytes 983040 | tf_op jit(solution)/shard_map/add | solution.py:441
Async XLA Ops:
  0.0 23.7 %copy-start = (f32[5,8,16,128]{3,2,1,0:T(8,128)S(1)}, f32[5,8,16,128]{3,2,1,0:T(8,128)}, u32[]{:S(2)}) copy-start(f32[5,8,16,128]{3,2,1,0:T(8,128)} %param.10) | copy-start | bytes 983044

commit v2 on v1

--- a/solution.py
+++ b/solution.py
@@ -19,6 +19,8 @@
 
 DIRS = ((-1, 0), (1, 0), (0, -1), (0, 1), (-1, -1), (-1, 1), (1, -1), (1, 1))
 OPPOSITE = (1, 0, 3, 2, 7, 6, 5, 4)
+DIRS_Z = DIRS + ((0, 0),)
+OPPOSITE_Z = OPPOSITE + (8,)
 
 
 def int_div(values, number):
@@ -42,6 +44,15 @@
 
 
 def kernel(
+    tile_in,
+    count_in,
+    gas_in,
+    cell_in,
+    frac_in,
+    vel_in,
+    mass_in,
+    temp_in,
+    out_ref,
     tile_ref,
     count_ref,
     gas_ref,
@@ -50,7 +61,7 @@
     vel_ref,
     mass_ref,
     temp_ref,
-    out_ref,
+    pick_ref,
     weight_ref,
     planar_ref,
     vert_ref,
@@ -73,6 +84,7 @@
     dxrecv_ref,
     dyrecv_ref,
     dcrecv_ref,
+    load_sem,
     send_sem,
     recv_sem,
 ):
@@ -82,8 +94,8 @@
     starts = (0, cy, 2 * cy, 2 * cy + cx)
     sizes = (cy, cy, cx, cx)
     corner_at = 2 * cy + 2 * cx
-    width = lhs_ref.shape[1]
-    used = dep_ref.shape[1]
+    width = planar_ref.shape[0]
+    used = plane + dep_ref.shape[1]
 
     ix, iy, iz = lax.axis_index("gx"), lax.axis_index("gy"), lax.axis_index("gz")
     nx, ny, nz = lax.axis_size("gx"), lax.axis_size("gy"), lax.axis_size("gz")
@@ -92,27 +104,49 @@
         dx, dy = DIRS[k]
         return {"gx": lax.rem(ix + dx + nx, nx), "gy": lax.rem(iy + dy + ny, ny), "gz": iz}
 
-    def z_id(side):
-        return {"gx": ix, "gy": iy, "gz": lax.rem(iz + (2 * side - 1) + nz, nz)}
+    def z_id(side, j):
+        dx, dy = DIRS_Z[j]
+        return {
+            "gx": lax.rem(ix + dx + nx, nx),
+            "gy": lax.rem(iy + dy + ny, ny),
+            "gz": lax.rem(iz + (2 * side - 1) + nz, nz),
+        }
+
+    pairs = (
+        (gas_in, gas_ref),
+        (cell_in, cell_ref),
+        (frac_in, frac_ref),
+        (tile_in, tile_ref),
+        (count_in, count_ref),
+        (vel_in, vel_ref),
+        (mass_in, mass_ref),
+        (temp_in, temp_ref),
+    )
+    loads = [
+        pltpu.make_async_copy(src, dst, load_sem.at[i]) for i, (src, dst) in enumerate(pairs)
+    ]
+    for load in loads:
+        load.start()
 
     barrier = pltpu.get_barrier_semaphore()
     for k in range(8):
         pl.semaphore_signal(barrier, inc=1, device_id=xy_id(k), device_id_type=MESH)
     for side in range(2):
-        pl.semaphore_signal(barrier, inc=1, device_id=z_id(side), device_id_type=MESH)
+        for j in range(9):
+            pl.semaphore_signal(barrier, inc=1, device_id=z_id(side, j), device_id_type=MESH)
 
     csend_ref[...] = jnp.zeros_like(csend_ref)
     zsend_ref[...] = jnp.zeros_like(zsend_ref)
     ghost_ref[:, corner_at:, :] = jnp.zeros(
         (comps, ghost_ref.shape[1] - corner_at, cz), F32
     )
+    for load in loads:
+        load.wait()
     ysend_ref[0] = gas_ref[:, :, 0, :]
     ysend_ref[1] = gas_ref[:, :, cy - 1, :]
     for j in range(4):
         dx, dy = DIRS[4 + j]
         csend_ref[j, :comps, :] = gas_ref[:, 0 if dx < 0 else cx - 1, 0 if dy < 0 else cy - 1, :]
-
-    pl.semaphore_wait(barrier, 10)
 
     def xy_copy(k, base, src, dst):
         return pltpu.make_async_remote_copy(
@@ -123,23 +157,6 @@
             device_id=xy_id(k),
             device_id_type=MESH,
         )
-
-    halo = []
-    for k in (4, 5, 6, 7, 0, 1, 2, 3):
-        other = OPPOSITE[k]
-        if k < 2:
-            src = gas_ref.at[:, 0 if k == 0 else cx - 1]
-        elif k < 4:
-            src = ysend_ref.at[k - 2]
-        else:
-            src = csend_ref.at[k - 4]
-        if k < 4:
-            dst = ghost_ref.at[:, pl.ds(starts[other], sizes[other])]
-        else:
-            dst = crecv_ref.at[other - 4]
-        copy = xy_copy(k, 0, src, dst)
-        copy.start()
-        halo.append(copy)
 
     cells = cell_ref[...]
     weight_ref[0] = int_div(cells, TS * cz).astype(F32)
@@ -199,39 +216,69 @@
 
     for c in range(comps):
         turned = gas_ref[c].reshape(plane, cz).T
-        lhs_ref[c * cz : (c + 1) * cz, :plane] = turned.astype(BF16)
-        zsend_ref[0, c : c + 1, :plane] = turned[0:1]
-        zsend_ref[1, c : c + 1, :plane] = turned[cz - 1 : cz]
-
-    for copy in halo:
-        copy.wait_recv()
-
-    for c in range(comps):
-        ghost_ref[c, corner_at : corner_at + 4, :] = crecv_ref[:, c, :]
-        turned = ghost_ref[c].T
-        lhs_ref[c * cz : (c + 1) * cz, plane:] = turned.astype(BF16)
-        zsend_ref[0, c : c + 1, plane:] = turned[0:1]
-        zsend_ref[1, c : c + 1, plane:] = turned[cz - 1 : cz]
-
-    def z_copy(side, base, src, dst):
-        return pltpu.make_async_remote_copy(
-            src_ref=src.at[side],
-            dst_ref=dst.at[1 - side],
-            send_sem=send_sem.at[base + side],
-            recv_sem=recv_sem.at[base + 1 - side],
-            device_id=z_id(side),
-            device_id_type=MESH,
-        )
-
-    z_halo = [z_copy(side, 8, zsend_ref, zrecv_ref) for side in range(2)]
-    for copy in z_halo:
+        lhs_ref[c * cz : (c + 1) * cz, :] = turned.astype(BF16)
+        zsend_ref[0, c : c + 1, :] = turned[0:1]
+        zsend_ref[1, c : c + 1, :] = turned[cz - 1 : cz]
+
+    cell_id = lax.broadcasted_iota(jnp.int32, (plane, LANES), 0)
+    ring_id = lax.broadcasted_iota(jnp.int32, (plane, LANES), 1)
+    for k in range(8):
+        dx, dy = DIRS[k]
+        if k < 4:
+            step = ring_id - starts[k]
+            inside = (step >= 0) & (step < sizes[k])
+            if k < 2:
+                wanted = step + (cx - 1 if dx < 0 else 0) * cy
+            else:
+                wanted = step * cy + (cy - 1 if dy < 0 else 0)
+        else:
+            inside = ring_id == corner_at + k - 4
+            wanted = (cx - 1 if dx < 0 else 0) * cy + (cy - 1 if dy < 0 else 0)
+        hit = inside & (cell_id == wanted)
+        pick_ref[k * plane : (k + 1) * plane, :] = jnp.where(hit, 1.0, 0.0).astype(BF16)
+
+    def z_copies(base, source, dst):
+        copies = []
+        for j in range(9):
+            for side in range(2):
+                copies.append(
+                    pltpu.make_async_remote_copy(
+                        src_ref=source(side, j),
+                        dst_ref=dst.at[OPPOSITE_Z[j], 1 - side],
+                        send_sem=send_sem.at[base + 2 * j + side],
+                        recv_sem=recv_sem.at[base + 2 * OPPOSITE_Z[j] + 1 - side],
+                        device_id=z_id(side, j),
+                        device_id_type=MESH,
+                    )
+                )
+                copies[-1].start()
+        return copies
+
+    pl.semaphore_wait(barrier, 26)
+
+    z_halo = z_copies(8, lambda side, j: zsend_ref.at[side], zrecv_ref)
+    halo = []
+    for k in (4, 5, 6, 7, 0, 1, 2, 3):
+        other = OPPOSITE[k]
+        if k < 2:
+            src = gas_ref.at[:, 0 if k == 0 else cx - 1]
+        elif k < 4:
+            src = ysend_ref.at[k - 2]
+        else:
+            src = csend_ref.at[k - 4]
+        if k < 4:
+            dst = ghost_ref.at[:, pl.ds(starts[other], sizes[other])]
+        else:
+            dst = crecv_ref.at[other - 4]
+        copy = xy_copy(k, 0, src, dst)
         copy.start()
+        halo.append(copy)
 
     pair = 2 if blocks % 2 == 0 else 1
 
     def gather(i, carry):
         at = pl.ds(pl.multiple_of(i * pair * slots, pair * slots), pair * slots)
-        planar = planar_ref[:, at]
+        planar = planar_ref[:plane, at]
         vertical = vert_ref[:, at].astype(F32)
         for c in range(comps):
             near = jnp.dot(
@@ -244,16 +291,33 @@
 
     lax.fori_loop(0, blocks // pair, gather, 0)
 
-    for copy in z_halo:
+    for copy in halo + z_halo:
         copy.wait_recv()
 
-    z_values = jnp.concatenate([zrecv_ref[0], zrecv_ref[1]], axis=0).astype(BF16)
-    near_ends = jnp.dot(z_values, planar_ref[...], preferred_element_type=F32)
-    for b in range(blocks):
-        part = near_ends[:, b * slots : (b + 1) * slots]
-        both = part[:8] * vghost_ref[b, 0:1, :] + part[8:] * vghost_ref[b, 1:2, :]
+    for c in range(comps):
+        ghost_ref[c, corner_at : corner_at + 4, :] = crecv_ref[:, c, :]
+    ring = jnp.concatenate(
+        [zrecv_ref[j].reshape(16, plane).astype(BF16) for j in range(8)], axis=1
+    )
+    ring = jnp.dot(ring, pick_ref[...], preferred_element_type=F32)
+    z_values = jnp.concatenate([zrecv_ref[8].reshape(16, plane), ring], axis=1).astype(BF16)
+
+    def gather_ghosts(i, carry):
+        at = pl.ds(pl.multiple_of(i * pair * slots, pair * slots), pair * slots)
+        planar = planar_ref[plane:used, at].astype(F32)
+        vertical = vert_ref[:, at]
+        near_ends = jnp.dot(z_values, planar_ref[:, at], preferred_element_type=F32)
+        low = jnp.concatenate([vghost_ref[i * pair + j, 0:1, :] for j in range(pair)], axis=1)
+        high = jnp.concatenate([vghost_ref[i * pair + j, 1:2, :] for j in range(pair)], axis=1)
+        both = near_ends[:8] * low + near_ends[8:] * high
         for c in range(comps):
-            gasat_ref[c, b : b + 1, :] += both[c : c + 1]
+            near = jnp.dot(ghost_ref[c].astype(BF16), vertical, preferred_element_type=F32)
+            value = jnp.sum(near * planar, axis=0, keepdims=True) + both[c : c + 1]
+            for j in range(pair):
+                gasat_ref[c, pl.ds(i * pair + j, 1), :] += value[:, j * slots : (j + 1) * slots]
+        return carry
+
+    lax.fori_loop(0, blocks // pair, gather_ghosts, 0)
 
     temper = temp_ref[...]
     diameter = jnp.exp(jnp.log(mass_ref[...]) * (1.0 / 3.0))
@@ -291,51 +355,44 @@
         return lax.dot_general(lhs, rhs, (((1,), (1,)), ((), ())), preferred_element_type=F32)
 
     z_ends = contract(sghost_ref[...], planar_ref[...])
-    dzsend_ref[0] = z_ends[:8]
-    dzsend_ref[1] = z_ends[8:]
-    z_deposit = [z_copy(side, 10, dzsend_ref, dzrecv_ref) for side in range(2)]
-    for copy in z_deposit:
-        copy.start()
-
-    for c in range(comps):
-        dep_ref[c] = contract(planar_ref[:used, :], scaled_ref[c * cz : (c + 1) * cz, :])
-
-    for copy in z_deposit:
-        copy.wait_recv()
-
-    lane = lax.broadcasted_iota(jnp.int32, (plane, cz), 1)
-    row_y = int_mod(lax.broadcasted_iota(jnp.int32, (plane, cz), 0), cy)
-
-    def columns(ref, first):
-        both = jnp.concatenate([ref[0], ref[1]], axis=0)[:, first : first + LANES]
-        return jnp.concatenate([both, jnp.zeros((LANES - 16, LANES), F32)], axis=0).T
-
-    def at_ends(turned, rows, c):
-        lanes = lax.broadcasted_iota(jnp.int32, (rows, cz), 1)
-        low, high = turned[:rows, c : c + 1], turned[:rows, 8 + c : 9 + c]
-        return jnp.where(lanes == 0, low, 0.0) + jnp.where(lanes == cz - 1, high, 0.0)
-
-    outer = columns(dzrecv_ref, plane)
+    for side in range(2):
+        dzsend_ref[0, side] = z_ends[8 * side : 8 * side + 8, :plane]
+        dzsend_ref[1, side] = z_ends[8 * side : 8 * side + 8, plane:]
+    z_deposit = z_copies(34, lambda side, j: dzsend_ref.at[0 if j == 8 else 1, side], dzrecv_ref)
+
     dcsend_ref[...] = jnp.zeros_like(dcsend_ref)
     for c in range(comps):
-        dep_ref[c, plane:, :] += at_ends(outer, used - plane, c)
+        ghosts = contract(planar_ref[plane:used, :], scaled_ref[c * cz : (c + 1) * cz, :])
+        dep_ref[c] = ghosts
         for j in range(4):
-            dcsend_ref[j, c : c + 1, :] = dep_ref[c, plane + corner_at + j : plane + corner_at + j + 1, :]
+            dcsend_ref[j, c : c + 1, :] = ghosts[corner_at + j : corner_at + j + 1]
 
     deposit = []
     for k in (4, 5, 6, 7, 0, 1, 2, 3):
         other = OPPOSITE[k]
         if k < 4:
-            src = dep_ref.at[:, pl.ds(plane + starts[k], sizes[k])]
+            src = dep_ref.at[:, pl.ds(starts[k], sizes[k])]
             dst = (dxrecv_ref if k < 2 else dyrecv_ref).at[other % 2]
         else:
             src, dst = dcsend_ref.at[k - 4], dcrecv_ref.at[other - 4]
-        copy = xy_copy(k, 12, src, dst)
+        copy = xy_copy(k, 26, src, dst)
         copy.start()
         deposit.append(copy)
 
-    inner = columns(dzrecv_ref, 0)
-    z_sides = columns(zrecv_ref, 0)
+    lane = lax.broadcasted_iota(jnp.int32, (plane, cz), 1)
+    row_y = int_mod(lax.broadcasted_iota(jnp.int32, (plane, cz), 0), cy)
+
+    def columns(ref):
+        both = ref[8].reshape(16, plane)
+        return jnp.concatenate([both, jnp.zeros((LANES - 16, plane), F32)], axis=0).T
+
+    def at_ends(turned, first, rows, at):
+        lanes = lax.broadcasted_iota(jnp.int32, (rows, cz), 1)
+        low = turned[first : first + rows, at : at + 1]
+        high = turned[first : first + rows, 8 + at : 9 + at]
+        return jnp.where(lanes == 0, low, 0.0) + jnp.where(lanes == cz - 1, high, 0.0)
+
+    z_sides = columns(zrecv_ref)
     flow = [gas_ref[1 + a].reshape(plane, cz) for a in range(3)]
     for c in range(comps):
         cube = gas_ref[c]
@@ -355,21 +412,30 @@
         advect = 0.5 * (
             flow[0] * (x_high - x_low) + flow[1] * (y_high - y_low) + flow[2] * (z_high - z_low)
         )
-        own = dep_ref[c, :plane, :] + at_ends(inner, plane, c)
+        own = contract(planar_ref[:plane, :], scaled_ref[c * cz : (c + 1) * cz, :])
         out_ref[c] = (q + TIME_INCREMENT * (VISCOSITY * laplace - advect + own)).reshape(cx, cy, cz)
 
-    for copy in deposit:
+    for copy in z_deposit + deposit:
         copy.wait_recv()
 
+    inner = columns(dzrecv_ref)
+    outer = jnp.concatenate([dzrecv_ref[j].reshape(16, LANES) for j in range(8)], axis=0).T
     for c in range(comps):
+        ends_c = at_ends(inner, 0, plane, c)
+        out_ref[c] += TIME_INCREMENT * ends_c.reshape(cx, cy, cz)
         for side in range(2):
             x_at, y_at = (cx - 1) * side, (cy - 1) * side
-            out_ref[c, x_at] += TIME_INCREMENT * dxrecv_ref[side, c]
-            out_ref[c, :, y_at, :] += TIME_INCREMENT * dyrecv_ref[side, c]
+            x_ends = at_ends(outer, starts[1 - side], cy, 16 * side + c)
+            y_ends = at_ends(outer, starts[3 - side], cx, 16 * (2 + side) + c)
+            out_ref[c, x_at] += TIME_INCREMENT * (dxrecv_ref[side, c] + x_ends)
+            out_ref[c, :, y_at, :] += TIME_INCREMENT * (dyrecv_ref[side, c] + y_ends)
         for j in range(4):
             dx, dy = DIRS[4 + j]
             x_at, y_at = 0 if dx < 0 else cx - 1, 0 if dy < 0 else cy - 1
-            out_ref[c, x_at, y_at : y_at + 1, :] += TIME_INCREMENT * dcrecv_ref[j, c : c + 1, :]
+            corner = at_ends(outer, corner_at + OPPOSITE[4 + j] - 4, 1, 16 * (4 + j) + c)
+            out_ref[c, x_at, y_at : y_at + 1, :] += TIME_INCREMENT * (
+                dcrecv_ref[j, c : c + 1, :] + corner
+            )
 
     for copy in halo + z_halo + z_deposit + deposit:
         copy.wait_send()
@@ -394,38 +460,47 @@
     width = plane + ghost_width
     used = plane + -(-ghosts // 16) * 16
     total = blocks * slots
-    smem = pl.BlockSpec(memory_space=pltpu.SMEM)
     vmem = pl.BlockSpec(memory_space=pltpu.VMEM)
     section = pl.pallas_call(
         kernel,
         out_shape=jax.ShapeDtypeStruct(gas_state.shape, F32),
-        in_specs=[smem] * 2 + [vmem] * 6,
+        in_specs=[pl.BlockSpec(memory_space=pl.ANY)] * 8,
         out_specs=vmem,
         scratch_shapes=[
+            pltpu.SMEM((blocks,), jnp.int32),
+            pltpu.SMEM((blocks,), jnp.int32),
+            pltpu.VMEM(gas_state.shape, F32),
+            pltpu.VMEM((blocks, slots), jnp.int32),
+            pltpu.VMEM((3, blocks, slots), F32),
+            pltpu.VMEM((3, blocks, slots), F32),
+            pltpu.VMEM((blocks, slots), F32),
+            pltpu.VMEM((blocks, slots), F32),
+            pltpu.VMEM((8 * plane, ghost_width), BF16),
             pltpu.VMEM((12, blocks, slots), F32),
             pltpu.VMEM((width, total), BF16),
             pltpu.VMEM((cz, total), BF16),
             pltpu.VMEM((blocks, 8, slots), F32),
             pltpu.VMEM((comps * cz, total), BF16),
             pltpu.VMEM((16, total), BF16),
-            pltpu.VMEM((comps * cz, width), BF16),
-            pltpu.VMEM((comps, ghost_width, cz), F32),
+            pltpu.VMEM((comps * cz, plane), BF16),
+            pltpu.VMEM((comps, used - plane, cz), F32),
             pltpu.VMEM((2, comps, cx, cz), F32),
             pltpu.VMEM((4, 8, cz), F32),
             pltpu.VMEM((4, 8, cz), F32),
-            pltpu.VMEM((2, 8, width), F32),
-            pltpu.VMEM((2, 8, width), F32),
+            pltpu.VMEM((2, 8, plane), F32),
+            pltpu.VMEM((9, 2, 8, plane), F32),
             pltpu.VMEM((comps, blocks, slots), F32),
             pltpu.VMEM((comps, blocks, slots), F32),
-            pltpu.VMEM((comps, used, cz), F32),
+            pltpu.VMEM((comps, used - plane, cz), F32),
             pltpu.VMEM((4, 8, cz), F32),
-            pltpu.VMEM((2, 8, width), F32),
-            pltpu.VMEM((2, 8, width), F32),
+            pltpu.VMEM((2, 2, 8, ghost_width), F32),
+            pltpu.VMEM((9, 2, 8, ghost_width), F32),
             pltpu.VMEM((2, comps, cy, cz), F32),
             pltpu.VMEM((2, comps, cx, cz), F32),
             pltpu.VMEM((4, 8, cz), F32),
-            pltpu.SemaphoreType.DMA((20,)),
-            pltpu.SemaphoreType.DMA((20,)),
+            pltpu.SemaphoreType.DMA((8,)),
+            pltpu.SemaphoreType.DMA((52,)),
+            pltpu.SemaphoreType.DMA((52,)),
         ],
         compiler_params=pltpu.CompilerParams(collective_id=0, has_side_effects=True),
     )(

time: 25.6 us -> 24.9 us (0.973)
  Pallas kernels: 23.7 us -> 23 us
    pallas_call x1, Pallas kernels: 23.7 us -> 23 us  [local(): pl.pallas_call(kernel, out_shape=jax.ShapeDtypeStruct(gas_state.shape, F3...]
where the time goes in v2:
time: 24.9 us; the launch traced here: 24.7 us
  Pallas kernels  23 us (92%)
  other arithmetic  1.74 us (7%)
    pallas_call x1, Pallas kernels, local(): pl.pallas_call(kernel, out_shape=jax.ShapeDtypeStruct(gas_state.shape, F3...  23 us
    add x1, other arithmetic, local(): return 0.75 * section_start + 0.25 * section  1.74 us

profile of v2, /device:TPU:0, one launch (start us, length us, event | category | flops | bytes accessed | tf_op | source)
XLA Modules:
  0.0 24.7 jit_solution(9444681776146713962)
XLA Ops:
  0.0 0.0 copy-start
  0.0 23.0 %shard_map.91 = f32[5,8,16,128]{3,2,1,0:T(8,128)} custom-call(s32[16]{0:T(128)} %bitcast.12, s32[16]{0:T(128)} %bitcast.13, f32[5,8,16,128]{3,2,1,0:T(8,128)} %gas_in.1, s32[16,128]{1,0:T(8,128)} %bitcast.9, f32[3,16,128]{2,1,0:T(8,128)} %bitcast.7, f32[3,16,128]{2,1,0:T(8,128)} %bitcast.8, f32[16,128]{1,0:T(8,128)} %bitcast.10, f32[16,128]{1,0:T(8,128)} %bitcast.11), custom_call_target="tpu_custom_call" | custom-call | tf_op jit(solution)/shard_map/pallas_call | solution.py:464
  23.0 0.0 copy-done
  23.0 1.7 %multiply_add_fusion = f32[5,8,16,128]{3,2,1,0:T(8,128)} fusion(f32[5,8,16,128]{3,2,1,0:T(8,128)} %shard_map.91, f32[5,8,16,128]{3,2,1,0:T(8,128)S(1)} %copy-done), kind=kLoop, calls=%fused_computation | loop fusion | flops 245760 | bytes 983040 | tf_op jit(solution)/shard_map/add | solution.py:516
Async XLA Ops:
  0.0 23.0 %copy-start = (f32[5,8,16,128]{3,2,1,0:T(8,128)S(1)}, f32[5,8,16,128]{3,2,1,0:T(8,128)}, u32[]{:S(2)}) copy-start(f32[5,8,16,128]{3,2,1,0:T(8,128)} %param.10) | copy-start | bytes 983044

commit v3 on v2

--- a/solution.py
+++ b/solution.py
@@ -131,7 +131,8 @@
     barrier = pltpu.get_barrier_semaphore()
     for k in range(8):
         pl.semaphore_signal(barrier, inc=1, device_id=xy_id(k), device_id_type=MESH)
-    for side in range(2):
+    z_sides_apart = range(2) if nz > 2 else range(1)
+    for side in z_sides_apart:
         for j in range(9):
             pl.semaphore_signal(barrier, inc=1, device_id=z_id(side, j), device_id_type=MESH)
 
@@ -140,8 +141,7 @@
     ghost_ref[:, corner_at:, :] = jnp.zeros(
         (comps, ghost_ref.shape[1] - corner_at, cz), F32
     )
-    for load in loads:
-        load.wait()
+    loads[0].wait()
     ysend_ref[0] = gas_ref[:, :, 0, :]
     ysend_ref[1] = gas_ref[:, :, cy - 1, :]
     for j in range(4):
@@ -158,6 +158,53 @@
             device_id_type=MESH,
         )
 
+    for c in range(comps):
+        turned = gas_ref[c].reshape(plane, cz).T
+        lhs_ref[c * cz : (c + 1) * cz, :] = turned.astype(BF16)
+        zsend_ref[1, c : c + 1, :] = turned[0:1]
+        zsend_ref[0, c : c + 1, :] = turned[cz - 1 : cz]
+
+    def z_copies(base, source, dst):
+        copies = []
+        for j in range(9):
+            for side in z_sides_apart:
+                src, at = source(j), OPPOSITE_Z[j]
+                apart = len(z_sides_apart) == 2
+                copies.append(
+                    pltpu.make_async_remote_copy(
+                        src_ref=src.at[1 - side] if apart else src,
+                        dst_ref=dst.at[at, 1 - side] if apart else dst.at[at],
+                        send_sem=send_sem.at[base + 2 * j + side],
+                        recv_sem=recv_sem.at[base + 2 * at + (1 - side if apart else 0)],
+                        device_id=z_id(side, j),
+                        device_id_type=MESH,
+                    )
+                )
+                copies[-1].start()
+        return copies
+
+    pl.semaphore_wait(barrier, 8 + 9 * len(z_sides_apart))
+
+    z_halo = z_copies(8, lambda j: zsend_ref, zrecv_ref)
+    halo = []
+    for k in (4, 5, 6, 7, 0, 1, 2, 3):
+        other = OPPOSITE[k]
+        if k < 2:
+            src = gas_ref.at[:, 0 if k == 0 else cx - 1]
+        elif k < 4:
+            src = ysend_ref.at[k - 2]
+        else:
+            src = csend_ref.at[k - 4]
+        if k < 4:
+            dst = ghost_ref.at[:, pl.ds(starts[other], sizes[other])]
+        else:
+            dst = crecv_ref.at[other - 4]
+        copy = xy_copy(k, 0, src, dst)
+        copy.start()
+        halo.append(copy)
+
+    for load in loads[1:]:
+        load.wait()
     cells = cell_ref[...]
     weight_ref[0] = int_div(cells, TS * cz).astype(F32)
     weight_ref[1] = int_mod(int_div(cells, cz), TS).astype(F32)
@@ -214,12 +261,6 @@
 
     lax.fori_loop(0, blocks, make_weights, 0)
 
-    for c in range(comps):
-        turned = gas_ref[c].reshape(plane, cz).T
-        lhs_ref[c * cz : (c + 1) * cz, :] = turned.astype(BF16)
-        zsend_ref[0, c : c + 1, :] = turned[0:1]
-        zsend_ref[1, c : c + 1, :] = turned[cz - 1 : cz]
-
     cell_id = lax.broadcasted_iota(jnp.int32, (plane, LANES), 0)
     ring_id = lax.broadcasted_iota(jnp.int32, (plane, LANES), 1)
     for k in range(8):
@@ -237,54 +278,15 @@
         hit = inside & (cell_id == wanted)
         pick_ref[k * plane : (k + 1) * plane, :] = jnp.where(hit, 1.0, 0.0).astype(BF16)
 
-    def z_copies(base, source, dst):
-        copies = []
-        for j in range(9):
-            for side in range(2):
-                copies.append(
-                    pltpu.make_async_remote_copy(
-                        src_ref=source(side, j),
-                        dst_ref=dst.at[OPPOSITE_Z[j], 1 - side],
-                        send_sem=send_sem.at[base + 2 * j + side],
-                        recv_sem=recv_sem.at[base + 2 * OPPOSITE_Z[j] + 1 - side],
-                        device_id=z_id(side, j),
-                        device_id_type=MESH,
-                    )
-                )
-                copies[-1].start()
-        return copies
-
-    pl.semaphore_wait(barrier, 26)
-
-    z_halo = z_copies(8, lambda side, j: zsend_ref.at[side], zrecv_ref)
-    halo = []
-    for k in (4, 5, 6, 7, 0, 1, 2, 3):
-        other = OPPOSITE[k]
-        if k < 2:
-            src = gas_ref.at[:, 0 if k == 0 else cx - 1]
-        elif k < 4:
-            src = ysend_ref.at[k - 2]
-        else:
-            src = csend_ref.at[k - 4]
-        if k < 4:
-            dst = ghost_ref.at[:, pl.ds(starts[other], sizes[other])]
-        else:
-            dst = crecv_ref.at[other - 4]
-        copy = xy_copy(k, 0, src, dst)
-        copy.start()
-        halo.append(copy)
-
     pair = 2 if blocks % 2 == 0 else 1
 
     def gather(i, carry):
         at = pl.ds(pl.multiple_of(i * pair * slots, pair * slots), pair * slots)
         planar = planar_ref[:plane, at]
         vertical = vert_ref[:, at].astype(F32)
+        near = jnp.dot(lhs_ref[...], planar, preferred_element_type=F32)
         for c in range(comps):
-            near = jnp.dot(
-                lhs_ref[c * cz : (c + 1) * cz, :], planar, preferred_element_type=F32
-            )
-            value = jnp.sum(near * vertical, axis=0, keepdims=True)
+            value = jnp.sum(near[c * cz : (c + 1) * cz] * vertical, axis=0, keepdims=True)
             for j in range(pair):
                 gasat_ref[c, pl.ds(i * pair + j, 1), :] = value[:, j * slots : (j + 1) * slots]
         return carry
@@ -301,6 +303,8 @@
     )
     ring = jnp.dot(ring, pick_ref[...], preferred_element_type=F32)
     z_values = jnp.concatenate([zrecv_ref[8].reshape(16, plane), ring], axis=1).astype(BF16)
+
+    ghost_rows = ghost_ref[...].reshape(comps * (used - plane), cz).astype(BF16)
 
     def gather_ghosts(i, carry):
         at = pl.ds(pl.multiple_of(i * pair * slots, pair * slots), pair * slots)
@@ -310,9 +314,10 @@
         low = jnp.concatenate([vghost_ref[i * pair + j, 0:1, :] for j in range(pair)], axis=1)
         high = jnp.concatenate([vghost_ref[i * pair + j, 1:2, :] for j in range(pair)], axis=1)
         both = near_ends[:8] * low + near_ends[8:] * high
+        near = jnp.dot(ghost_rows, vertical, preferred_element_type=F32)
         for c in range(comps):
-            near = jnp.dot(ghost_ref[c].astype(BF16), vertical, preferred_element_type=F32)
-            value = jnp.sum(near * planar, axis=0, keepdims=True) + both[c : c + 1]
+            part = near[c * (used - plane) : (c + 1) * (used - plane)]
+            value = jnp.sum(part * planar, axis=0, keepdims=True) + both[c : c + 1]
             for j in range(pair):
                 gasat_ref[c, pl.ds(i * pair + j, 1), :] += value[:, j * slots : (j + 1) * slots]
         return carry
@@ -356,13 +361,14 @@
 
     z_ends = contract(sghost_ref[...], planar_ref[...])
     for side in range(2):
-        dzsend_ref[0, side] = z_ends[8 * side : 8 * side + 8, :plane]
-        dzsend_ref[1, side] = z_ends[8 * side : 8 * side + 8, plane:]
-    z_deposit = z_copies(34, lambda side, j: dzsend_ref.at[0 if j == 8 else 1, side], dzrecv_ref)
+        dzsend_ref[0, 1 - side] = z_ends[8 * side : 8 * side + 8, :plane]
+        dzsend_ref[1, 1 - side] = z_ends[8 * side : 8 * side + 8, plane:]
+    z_deposit = z_copies(34, lambda j: dzsend_ref.at[0 if j == 8 else 1], dzrecv_ref)
 
     dcsend_ref[...] = jnp.zeros_like(dcsend_ref)
+    all_ghosts = contract(planar_ref[plane:used, :], scaled_ref[...])
     for c in range(comps):
-        ghosts = contract(planar_ref[plane:used, :], scaled_ref[c * cz : (c + 1) * cz, :])
+        ghosts = all_ghosts[:, c * cz : (c + 1) * cz]
         dep_ref[c] = ghosts
         for j in range(4):
             dcsend_ref[j, c : c + 1, :] = ghosts[corner_at + j : corner_at + j + 1]
@@ -393,6 +399,7 @@
         return jnp.where(lanes == 0, low, 0.0) + jnp.where(lanes == cz - 1, high, 0.0)
 
     z_sides = columns(zrecv_ref)
+    all_own = contract(planar_ref[:plane, :], scaled_ref[...])
     flow = [gas_ref[1 + a].reshape(plane, cz) for a in range(3)]
     for c in range(comps):
         cube = gas_ref[c]
@@ -412,7 +419,7 @@
         advect = 0.5 * (
             flow[0] * (x_high - x_low) + flow[1] * (y_high - y_low) + flow[2] * (z_high - z_low)
         )
-        own = contract(planar_ref[:plane, :], scaled_ref[c * cz : (c + 1) * cz, :])
+        own = all_own[:, c * cz : (c + 1) * cz]
         out_ref[c] = (q + TIME_INCREMENT * (VISCOSITY * laplace - advect + own)).reshape(cx, cy, cz)
 
     for copy in z_deposit + deposit:
@@ -463,7 +470,7 @@
     vmem = pl.BlockSpec(memory_space=pltpu.VMEM)
     section = pl.pallas_call(
         kernel,
-        out_shape=jax.ShapeDtypeStruct(gas_state.shape, F32),
+        out_shape=pltpu.VMEM(gas_state.shape, F32),
         in_specs=[pl.BlockSpec(memory_space=pl.ANY)] * 8,
         out_specs=vmem,
         scratch_shapes=[

time: 24.9 us -> 23.1 us (0.928)
  other arithmetic: 1.74 us -> 0.77 us
  Pallas kernels: 23 us -> 22.1 us
    add x1, other arithmetic: 1.74 us -> 0.77 us  [local(): return 0.75 * section_start + 0.25 * section]
    pallas_call x1, Pallas kernels: 23 us -> 22.1 us  [local(): pl.pallas_call(kernel, out_shape=pltpu.VMEM(gas_state.shape, F32), in_spe...]
where the time goes in v3:
time: 23.1 us; the launch traced here: 22.9 us
  Pallas kernels  22.1 us (96%)
  other arithmetic  0.77 us (3%)
    pallas_call x1, Pallas kernels, local(): pl.pallas_call(kernel, out_shape=pltpu.VMEM(gas_state.shape, F32), in_spe...  22.1 us
    add x1, other arithmetic, local(): return 0.75 * section_start + 0.25 * section  0.77 us

profile of v3, /device:TPU:0, one launch (start us, length us, event | category | flops | bytes accessed | tf_op | source)
XLA Modules:
  0.0 22.9 jit_solution(11743192440838171175)
XLA Ops:
  0.0 0.0 copy-start
  0.0 22.1 %shard_map.91 = f32[5,8,16,128]{3,2,1,0:T(8,128)S(1)} custom-call(s32[16]{0:T(128)} %bitcast.12, s32[16]{0:T(128)} %bitcast.13, f32[5,8,16,128]{3,2,1,0:T(8,128)} %gas_in.1, s32[16,128]{1,0:T(8,128)} %bitcast.9, f32[3,16,128]{2,1,0:T(8,128)} %bitcast.7, f32[3,16,128]{2,1,0:T(8,128)} %bitcast.8, f32[16,128]{1,0:T(8,128)} %bitcast.10, f32[16,128]{1,0:T(8,128)} %bitcast.11), custom_call_target="tpu_custom_call" | custom-call | tf_op jit(solution)/shard_map/pallas_call | solution.py:471
  22.1 0.0 copy-done
  22.2 0.8 %multiply_add_fusion = f32[5,8,16,128]{3,2,1,0:T(8,128)} fusion(f32[5,8,16,128]{3,2,1,0:T(8,128)S(1)} %shard_map.91, f32[5,8,16,128]{3,2,1,0:T(8,128)S(1)} %copy-done), kind=kLoop, calls=%fused_computation | loop fusion | flops 245760 | bytes 983040 | tf_op jit(solution)/shard_map/add | solution.py:523
Async XLA Ops:
  0.0 22.2 %copy-start = (f32[5,8,16,128]{3,2,1,0:T(8,128)S(1)}, f32[5,8,16,128]{3,2,1,0:T(8,128)}, u32[]{:S(2)}) copy-start(f32[5,8,16,128]{3,2,1,0:T(8,128)} %param.10) | copy-start | bytes 983044

commit v4 on v3

--- a/solution.py
+++ b/solution.py
@@ -259,7 +259,7 @@
         vghost_ref[b] = tap(ends(cz), anchor_z, *tz).astype(BF16).astype(F32)
         return carry
 
-    lax.fori_loop(0, blocks, make_weights, 0)
+    lax.fori_loop(0, blocks, make_weights, 0, unroll=4)
 
     cell_id = lax.broadcasted_iota(jnp.int32, (plane, LANES), 0)
     ring_id = lax.broadcasted_iota(jnp.int32, (plane, LANES), 1)
@@ -291,7 +291,7 @@
                 gasat_ref[c, pl.ds(i * pair + j, 1), :] = value[:, j * slots : (j + 1) * slots]
         return carry
 
-    lax.fori_loop(0, blocks // pair, gather, 0)
+    lax.fori_loop(0, blocks // pair, gather, 0, unroll=2)
 
     for copy in halo + z_halo:
         copy.wait_recv()
@@ -322,7 +322,7 @@
                 gasat_ref[c, pl.ds(i * pair + j, 1), :] += value[:, j * slots : (j + 1) * slots]
         return carry
 
-    lax.fori_loop(0, blocks // pair, gather_ghosts, 0)
+    lax.fori_loop(0, blocks // pair, gather_ghosts, 0, unroll=8)
 
     temper = temp_ref[...]
     diameter = jnp.exp(jnp.log(mass_ref[...]) * (1.0 / 3.0))
@@ -354,7 +354,7 @@
         sghost_ref[:, at] = jnp.concatenate([strengths * low, strengths * high], axis=0).astype(BF16)
         return carry
 
-    lax.fori_loop(0, blocks, scale, 0)
+    lax.fori_loop(0, blocks, scale, 0, unroll=4)
 
     def contract(lhs, rhs):
         return lax.dot_general(lhs, rhs, (((1,), (1,)), ((), ())), preferred_element_type=F32)

time: 23.1 us -> 21.9 us (0.948)
  Pallas kernels: 22.1 us -> 21 us
    pallas_call x1, Pallas kernels: 22.1 us -> 21 us  [local(): pl.pallas_call(kernel, out_shape=pltpu.VMEM(gas_state.shape, F32), in_spe...]
where the time goes in v4:
time: 21.9 us; the launch traced here: 21.8 us
  Pallas kernels  21 us (96%)
  other arithmetic  0.77 us (4%)
    pallas_call x1, Pallas kernels, local(): pl.pallas_call(kernel, out_shape=pltpu.VMEM(gas_state.shape, F32), in_spe...  21 us
    add x1, other arithmetic, local(): return 0.75 * section_start + 0.25 * section  0.77 us

profile of v4, /device:TPU:0, one launch (start us, length us, event | category | flops | bytes accessed | tf_op | source)
XLA Modules:
  0.0 21.8 jit_solution(13338678985722997210)
XLA Ops:
  0.0 0.0 copy-start
  0.0 21.0 %shard_map.91 = f32[5,8,16,128]{3,2,1,0:T(8,128)S(1)} custom-call(s32[16]{0:T(128)} %bitcast.12, s32[16]{0:T(128)} %bitcast.13, f32[5,8,16,128]{3,2,1,0:T(8,128)} %gas_in.1, s32[16,128]{1,0:T(8,128)} %bitcast.9, f32[3,16,128]{2,1,0:T(8,128)} %bitcast.7, f32[3,16,128]{2,1,0:T(8,128)} %bitcast.8, f32[16,128]{1,0:T(8,128)} %bitcast.10, f32[16,128]{1,0:T(8,128)} %bitcast.11), custom_call_target="tpu_custom_call" | custom-call | tf_op jit(solution)/shard_map/pallas_call | solution.py:471
  21.0 0.0 copy-done
  21.0 0.8 %multiply_add_fusion = f32[5,8,16,128]{3,2,1,0:T(8,128)} fusion(f32[5,8,16,128]{3,2,1,0:T(8,128)S(1)} %shard_map.91, f32[5,8,16,128]{3,2,1,0:T(8,128)S(1)} %copy-done), kind=kLoop, calls=%fused_computation | loop fusion | flops 245760 | bytes 983040 | tf_op jit(solution)/shard_map/add | solution.py:523
Async XLA Ops:
  0.0 21.0 %copy-start = (f32[5,8,16,128]{3,2,1,0:T(8,128)S(1)}, f32[5,8,16,128]{3,2,1,0:T(8,128)}, u32[]{:S(2)}) copy-start(f32[5,8,16,128]{3,2,1,0:T(8,128)} %param.10) | copy-start | bytes 983044
